TPU v7x, 512 devices: a whole 4x8x8 slice. The times are simulated.
512 devices in a mesh: pitch: 32 (over x, z), span: 8 (over y), row: 2 (over core).
Axes of the slice: x: 4, y: 8, z: 8, core: 2. Of those that a mesh axis runs over, the one named last changes fastest.
Arguments:
- fields: float32 [3, 512, 128, 512], P(None, 'pitch', 'span', 'row'), may hold values from -6 to 6
- diffusivity: float32 [512, 128, 512], P('pitch', 'span', 'row'), may hold values from 0.01 to 0.1
- mean_flow: bfloat16 [128, 2, 512], P('span', None, 'row'), may hold values from -6 to 6
- radial_kernel: bfloat16 [128, 128], replicated
- tracer_values: float32 [10, 1048576], P(None, ('pitch', 'span', 'row')), may hold values from -6 to 6
- tracer_cells: int32 [1048576], P(('pitch', 'span', 'row')), may hold values from 0 to 65535
- tracer_dest: int32 [1048576, 1], P(('pitch', 'span', 'row')), may hold values from 0 to 31; in each aligned block of 2048 rows (0 to 2047, 2048 to 4095, ...) at most 128 rows name the same one
- interface_map: int32 [2, 512], P('row', 'pitch'), may hold values from 0 to 511, as said below
Outputs:
- advected: float32 [3, 512, 128, 512], P(None, 'pitch', 'span', 'row')
- arrived: float32 [10, 2097152], P(None, ('pitch', 'span', 'row'))
Inputs may be any that keep to these rules, and one draw needn't show every extreme that they name: `tracer_cells`: the local index of the owning cell within the block of the device that holds the tracer, i * 16 * 256 + r * 256 + a for local indices i, r, a. `tracer_dest`: at most 128 of the tracers of one device go to one pitch index. `interface_map`: for one offset o of each draw, row 0 holds (i + o) mod 512 and row 1 holds (i - o) mod 512, so the two rows are inverse permutations.
All inputs are finite; a program needn't handle non-finite values.
Results may differ from a plain program's by a relative error of at most 0.0015.
Values may be sent and summed in bfloat16 or wider, within the bound.
A program may use at most 128 MiB of HBM per device.

v0:
```python
import jax
import jax.numpy as jnp
from jax import lax
from jax.sharding import PartitionSpec as P

SUB = 2


TIME_STEP = 0.9
AXIAL_SPEED = 0.15
PITCH_SPEED = 0.15


def swapped(block, axis, apart):
    count = lax.axis_size(axis)
    route = []
    for low in range(count):
        high = low | 1 << apart
        if high != low and high < count:
            route += [(low, high), (high, low)]
    return lax.ppermute(block, axis, route)


def padded(cells, sides, width):
    for axis, dim in sides:
        count = lax.axis_size(axis)
        head = lax.slice_in_dim(cells, 0, width, axis=dim)
        tail = lax.slice_in_dim(cells, cells.shape[dim] - width, cells.shape[dim], axis=dim)
        cells = jnp.concatenate(
            [
                lax.ppermute(tail, axis, [(i, (i + 1) % count) for i in range(count)]),
                cells,
                lax.ppermute(head, axis, [((i + 1) % count, i) for i in range(count)]),
            ],
            axis=dim,
        )
    return cells


def face_flux(left_values, right_values, left_kappa, right_kappa, face_speed):
    diffusion = -0.5 * (left_kappa + right_kappa) * (right_values - left_values)
    if face_speed is None:
        return diffusion
    return (
        jnp.maximum(face_speed, 0.0) * left_values
        + jnp.minimum(face_speed, 0.0) * right_values
        + diffusion
    )


def interface_ghost(own_face, local_map):
    across = swapped(own_face, "row", 0)
    picked = lax.all_gather(across, "pitch", axis=1, tiled=True)
    return jnp.take(picked, local_map, axis=1)


def update_core(extended, speed_axial, speed_pitch, ghost_face, wall_mask, row_id):
    along_pitch = extended[:, :, 1:-1, :]
    pitch_flux = face_flux(
        along_pitch[:3, :-1],
        along_pitch[:3, 1:],
        along_pitch[3, :-1],
        along_pitch[3, 1:],
        speed_pitch,
    )
    along_radius = extended[:, 1:-1]
    radial_flux = (
        face_flux(
            along_radius[:3, :, :-1],
            along_radius[:3, :, 1:],
            along_radius[3, :, :-1],
            along_radius[3, :, 1:],
            None,
        )
        * wall_mask[:, None]
    )
    core = extended[:, 1:-1, 1:-1]
    pitch_cells = core.shape[1]
    full_stack = jnp.concatenate(
        [core, jnp.broadcast_to(speed_axial[None, None], (1, pitch_cells) + speed_axial.shape)], 0
    )
    upstream = jnp.where(row_id == 0, full_stack[..., 0], ghost_face)
    downstream = jnp.where(row_id == 0, ghost_face, full_stack[..., -1])
    line = jnp.concatenate([upstream[..., None], full_stack, downstream[..., None]], -1)
    face_speed = 0.5 * (line[4, ..., :-1] + line[4, ..., 1:])
    axial_flux = face_flux(
        line[:3, ..., :-1], line[:3, ..., 1:], line[3, ..., :-1], line[3, ..., 1:], face_speed
    )
    divergence = (
        pitch_flux[:, 1:]
        - pitch_flux[:, :-1]
        + radial_flux[:, :, 1:]
        - radial_flux[:, :, :-1]
        + axial_flux[..., 1:]
        - axial_flux[..., :-1]
    )
    return core[:3] - TIME_STEP * divergence


def advance(state, diffusivity, speed_axial, speed_pitch, local_map, wall_mask):
    pitch_cells = state.shape[1]
    stacked = jnp.concatenate([state, diffusivity[None]], 0)
    extended = padded(stacked, (("pitch", 1), ("span", 2)), 1)
    full_stack = jnp.concatenate(
        [stacked, jnp.broadcast_to(speed_axial[None, None], (1, pitch_cells) + speed_axial.shape)],
        0,
    )
    row_id = lax.axis_index("row")
    own_face = jnp.where(row_id == 0, full_stack[..., -1], full_stack[..., 0])
    ghost_face = interface_ghost(own_face, local_map)
    return update_core(extended, speed_axial, speed_pitch, ghost_face, wall_mask, row_id)


def local(
    fields,
    diffusivity,
    mean_flow,
    radial_kernel,
    tracer_values,
    tracer_cells,
    tracer_dest,
    interface_map,
):
    radial_cells = mean_flow.shape[0]
    axial_cells = mean_flow.shape[2]
    flat_width = 2 * axial_cells
    span_id = lax.axis_index("span")
    kernel_cols = lax.dynamic_slice_in_dim(radial_kernel, span_id * radial_cells, radial_cells, 1)
    flat_rows = mean_flow.reshape(radial_cells, flat_width)
    smoothed = lax.psum_scatter(
        jnp.dot(kernel_cols, flat_rows, preferred_element_type=jnp.float32),
        "span",
        scatter_dimension=0,
        tiled=True,
    )
    smoothed = smoothed.reshape(radial_cells, 2, axial_cells)
    speed_axial = AXIAL_SPEED * (1.0 + 0.5 * jnp.tanh(smoothed[:, 0]))
    speed_pitch = PITCH_SPEED * jnp.tanh(smoothed[:, 1])
    plane_size = radial_cells * axial_cells
    sample_fields = jnp.take(fields.reshape(fields.shape[0], -1), tracer_cells, axis=1)
    sample_speed = jnp.take(
        jnp.stack([speed_axial, speed_pitch]).reshape(2, plane_size),
        tracer_cells % plane_size,
        axis=1,
    )
    sampled = jnp.concatenate([sample_fields, sample_speed], 0)
    head_rows = tracer_values[:5]
    tail_rows = tracer_values[5:]
    updated = jnp.concatenate(
        [head_rows + 0.5 * (sampled - head_rows), tail_rows + 0.8 * sampled], 0
    )
    npitch = lax.axis_size("pitch")
    capacity = 2 * tracer_values.shape[1] // npitch
    targets = tracer_dest[:, 0]
    onehot = (targets[:, None] == jnp.arange(npitch, dtype=jnp.int32)[None]).astype(jnp.int32)
    slot_index = jnp.sum((jnp.cumsum(onehot, 0) - onehot) * onehot, 1)
    position = targets * capacity + slot_index
    outgoing = (
        jnp.zeros((tracer_values.shape[0], npitch * capacity), jnp.float32)
        .at[:, position]
        .set(updated)
    )
    arrived = lax.all_to_all(outgoing, "pitch", split_axis=1, concat_axis=1, tiled=True)
    face_index = span_id * radial_cells + jnp.arange(radial_cells + 1, dtype=jnp.int32)
    total_radial = radial_cells * lax.axis_size("span")
    wall_mask = ((face_index > 0) & (face_index < total_radial)).astype(jnp.float32)
    local_map = interface_map[0]
    current = fields
    for substep in range(SUB):
        current = advance(current, diffusivity, speed_axial, speed_pitch, local_map, wall_mask)
    return (current, arrived)


def solution(mesh):
    placed = (
        P(None, "pitch", "span", "row"),
        P("pitch", "span", "row"),
        P("span", None, "row"),
        P(),
        P(None, ("pitch", "span", "row")),
        P(("pitch", "span", "row")),
        P(("pitch", "span", "row"), None),
        P("row", "pitch"),
    )
    return jax.shard_map(
        local,
        mesh=mesh,
        in_specs=placed,
        out_specs=(P(None, "pitch", "span", "row"), P(None, ("pitch", "span", "row"))),
        check_vma=False,
    )
```

profile of v0, /device:TPU:24, one launch (start us, length us, event | category | flops | bytes accessed | tf_op | source)
XLA Modules:
  0.0 287.4 jit_solution(10924218289385498217)
XLA Ops:
  7.2 1.1 copy.928
  8.4 1.3 constant_dynamic-update-slice_fusion
  9.8 0.7 fusion.65
  10.5 4.3 %collective-permute-start = (f32[4,1,16,256]{3,2,1,0:T(8,128)}, f32[4,1,16,256]{3,2,1,0:T(8,128)S(1)}, u32[]{:S(2)}, u32[]{:S(2)}) collective-permute-start(f32[4,1,16,256]{3,2,1,0:T(8,128)} %get-tuple-element.57), channel_id=1, source_target_pairs={{0,16},{16,32},{32,48},{48,64},{64,80},{80,96},{96,112},{112,128},... | collective-permute-start | bytes 196616 | tf_op jit(solution)/shard_map/ppermute | solution.py:31
  14.7 10.8 %collective-permute-start.1 = (f32[4,1,16,256]{3,2,1,0:T(8,128)}, f32[4,1,16,256]{3,2,1,0:T(8,128)}, u32[]{:S(2)}, u32[]{:S(2)}) collective-permute-start(f32[4,1,16,256]{3,2,1,0:T(8,128)} %get-tuple-element.58), channel_id=1, source_target_pairs={{16,0},{32,16},{48,32},{64,48},{80,64},{96,80},{112,96},{128,112},... | collective-permute-start | bytes 196616 | tf_op jit(solution)/shard_map/ppermute | solution.py:33
  25.6 0.9 fusion.48
  27.0 0.7 compare_and_fusion.2
  27.7 16.7 %copy.818 = f32[3,16,16,256]{0,3,2,1:T(8,128)} copy(f32[3,16,16,256]{3,2,1,0:T(8,128)S(1)} %copy-done.2) | data formatting | bytes 1572864 | tf_op args[0]
  44.4 18.2 %gather_fusion = f32[2048,3]{1,0:T(8,128)} fusion(f32[3,65536]{0,1:T(8,128)} %bitcast.121, s32[2048]{0:T(1024)S(1)} %get-tuple-element.74), kind=kCustom, calls=%fused_computation.2 | custom fusion | bytes 57344 | tf_op jit(solution)/shard_map/jit(_take)/gather | solution.py:140
  62.6 2.6 select_bitcast_fusion.1
  65.2 2.2 copy.820
  67.3 9.1 %reduce-window.6 = s32[32,16,128]{2,1,0:T(8,128)S(1)} reduce-window(s32[32,16,128]{2,1,0:T(8,128)S(1)} %fusion.43, s32[]{:T(128)} %constant.30.clone.1), window={size=1x1x128 pad=0_0x0_0x127_0}, to_apply=%region_1.0 | reduce-window | flops 8323072 | bytes 524292 | tf_op jit(solution)/shard_map/reduce-window
  77.9 0.9 pad_maximum_fusion.12
  79.0 4.7 %collective-permute-start.2 = (f32[4,18,1,256]{3,0,2,1:T(4,128)S(1)}, f32[4,18,1,256]{3,0,2,1:T(4,128)S(1)}, u32[]{:S(2)}, u32[]{:S(2)}) collective-permute-start(f32[4,18,1,256]{3,0,2,1:T(4,128)S(1)} %copy.846), channel_id=1, source_target_pairs={{0,2},{2,4},{4,6},{6,8},{8,10},{10,12},{12,14},{14,0},{1,3},{3,5},... | collective-permute-start | bytes 221192 | tf_op jit(solution)/shard_map/ppermute | solution.py:31
  83.7 1.9 collective-permute-start.3
  85.7 2.2 fusion.14
  87.9 0.7 fusion.39
  88.6 0.9 copy.769
  89.6 0.7 copy_dynamic-update-slice_fusion.2
  90.3 0.9 collective-permute-done.3
  91.3 1.2 fusion.19
  92.5 0.8 reshape.138
  93.7 0.8 copy.826
  94.6 0.8 copy.827
  95.4 0.7 bitcast_select_fusion.5
  96.1 1.9 collective-permute-start.4
  98.1 0.6 copy.819
  98.8 7.6 %gather_fusion.1 = f32[2048,2]{1,0:T(8,128)} fusion(f32[2,4096]{0,1:T(8,128)S(1)} %copy.819, s32[2048]{0:T(1024)S(1)} %get-tuple-element.75), kind=kCustom, calls=%fused_computation.3 | custom fusion | bytes 40960 | tf_op jit(solution)/shard_map/jit(_take)/gather | solution.py:141
  106.4 1.6 select_bitcast_fusion
  108.4 1.3 copy.822
  109.8 6.5 %scatter_custom_fusion = f32[10,4096]{0,1:T(8,128)S(1)} fusion(s32[2048]{0:T(1024)} %bitcast.141, f32[2048,10]{1,0:T(8,128)} %copy.822, f32[]{:T(128)} %constant.45.clone.1), kind=kCustom, calls=%fused_computation.51 | custom fusion | bytes 164352 | tf_op jit(solution)/shard_map/scatter | solution.py:161
  116.2 1.3 copy.823
  117.6 5.2 %all-to-all-start = ((f32[10,32,128]{2,0,1:T(8,128)}), f32[10,32,128]{2,0,1:T(8,128)}, u32[]{:S(2)}, u32[]{:S(2)}) async-start(f32[10,32,128]{2,0,1:T(8,128)} %copy.823), calls=%async_computation.1 | async-start | bytes 524288 | tf_op jit(solution)/shard_map/all_to_all | solution.py:163
  122.8 2.5 fusion.5
  125.3 0.8 copy.782
  126.2 51.2 %all_gather.6 = f32[5,512,16]{2,1,0:T(8,128)S(1)} all-gather(f32[5,16,16]{2,1,0:T(8,128)S(1)} %copy.782), channel_id=1, replica_groups=mesh['pitch'=32,'span'=8,'row'=2] {'pitch'}, dimensions={1}, use_global_device_ids=true | all-gather | bytes 168960 | tf_op jit(solution)/shard_map/all_gather | solution.py:53
  177.3 2.2 copy.783
  179.5 2.8 gather_fusion.2
  182.4 1.5 fusion.46
  183.9 2.2 copy.786
  186.1 1.4 copy.789
  187.5 2.0 fusion.2
  189.9 0.9 copy-done.5
  190.8 0.8 fusion.23
  192.4 1.0 fusion.60
  193.4 1.9 copy.834
  195.3 0.8 copy.835
  196.2 1.9 collective-permute-start.9
  198.1 0.6 fusion.64
  198.8 2.7 collective-permute-start.5
  201.4 6.5 %collective-permute-start.6 = (f32[4,1,16,256]{3,2,1,0:T(8,128)S(1)}, f32[4,1,16,256]{3,2,1,0:T(8,128)S(1)}, u32[]{:S(2)}, u32[]{:S(2)}) collective-permute-start(f32[4,1,16,256]{3,2,1,0:T(8,128)S(1)} %get-tuple-element.54), channel_id=1, source_target_pairs={{16,0},{32,16},{48,32},{64,48},{80,64},{96,80},{112,96},{128,112},... | collective-permute-start | bytes 196616 | tf_op jit(solution)/shard_map/ppermute | solution.py:33
  208.0 47.9 %all_gather.7 = f32[5,512,16]{2,1,0:T(8,128)S(1)} all-gather(f32[5,16,16]{2,1,0:T(8,128)S(1)} %copy.807), channel_id=1, replica_groups=mesh['pitch'=32,'span'=8,'row'=2] {'pitch'}, dimensions={1}, use_global_device_ids=true | all-gather | bytes 168960 | tf_op jit(solution)/shard_map/all_gather | solution.py:53
  255.8 2.2 copy.808
  258.0 2.1 gather_fusion.3
  260.8 1.4 copy.814
  262.2 1.8 fusion.3
  264.8 4.3 %collective-permute-start.7 = (f32[4,18,1,256]{3,0,2,1:T(4,128)S(1)}, f32[4,18,1,256]{3,0,2,1:T(4,128)S(1)}, u32[]{:S(2)}, u32[]{:S(2)}) collective-permute-start(f32[4,18,1,256]{3,0,2,1:T(4,128)S(1)} %copy.851), channel_id=1, source_target_pairs={{0,2},{2,4},{4,6},{6,8},{8,10},{10,12},{12,14},{14,0},{1,3},{3,5},... | collective-permute-start | bytes 221192 | tf_op jit(solution)/shard_map/ppermute | solution.py:31
  269.0 2.1 collective-permute-start.8
  271.4 1.0 fusion.8
  272.5 0.7 copy_dynamic-update-slice_fusion
  273.2 3.3 %collective-permute-done.8 = f32[4,18,1,256]{3,0,2,1:T(4,128)S(1)} collective-permute-done((f32[4,18,1,256]{3,0,2,1:T(4,128)S(1)}, f32[4,18,1,256]{3,0,2,1:T(4,128)S(1)}, u32[]{:S(2)}, u32[]{:S(2)}) %collective-permute-start.8) | collective-permute-done | bytes 73760 | tf_op jit(solution)/shard_map/ppermute | solution.py:33
  277.4 1.3 copy.825
  278.7 1.0 copy.824
  279.7 0.9 copy.857
  (102 shorter events, 7.0 us)
Async XLA Ops:
  7.2 18.4 %copy-start = (bf16[128,128]{1,0:T(8,128)(2,1)S(1)}, bf16[128,128]{1,0:T(8,128)(2,1)}, u32[]{:S(2)}) copy-start(bf16[128,128]{1,0:T(8,128)(2,1)} %param.13) | copy-start | bytes 98308
  7.2 85.3 %reduce-scatter.2.cloned.1.call-start = ((), (), s32[]{:S(2)}) async-start(), calls=%async_computation.2 | async-start | bytes 294912 | tf_op jit(solution)/shard_map/reduce_scatter | solution.py:130
  8.3 17.2 %copy-start.12 = (bf16[16,2,256]{2,1,0:T(2,128)(2,1)S(1)}, bf16[16,2,256]{2,1,0:T(2,128)(2,1)}, u32[]{:S(2)}) copy-start(bf16[16,2,256]{2,1,0:T(2,128)(2,1)} %param.12) | copy-start | bytes 49156
  8.3 18.2 %copy-start.2 = (f32[3,16,16,256]{3,2,1,0:T(8,128)S(1)}, f32[3,16,16,256]{3,2,1,0:T(8,128)}, u32[]{:S(2)}) copy-start(f32[3,16,16,256]{3,2,1,0:T(8,128)} %param.10) | copy-start | bytes 2359300
  9.8 17.2 %copy-start.16 = (s32[1,16]{1,0:T(1,128)S(1)}, s32[1,16]{1,0:T(1,128)}, u32[]{:S(2)}) copy-start(s32[1,16]{1,0:T(1,128)} %param.17) | copy-start | bytes 196
  9.8 17.9 %copy-start.11 = (s32[2048]{0:T(1024)S(1)}, s32[2048]{0:T(1024)}, u32[]{:S(2)}) copy-start(s32[2048]{0:T(1024)} %param.15) | copy-start | bytes 24580
  10.5 67.4 %collective-permute-start = (f32[4,1,16,256]{3,2,1,0:T(8,128)}, f32[4,1,16,256]{3,2,1,0:T(8,128)S(1)}, u32[]{:S(2)}, u32[]{:S(2)}) collective-permute-start(f32[4,1,16,256]{3,2,1,0:T(8,128)} %get-tuple-element.57), channel_id=1, source_target_pairs={{0,16},{16,32},{32,48},{48,64},{64,80},{80,96},{96,112},{112,128},... | collective-permute-start | bytes 196616 | tf_op jit(solution)/shard_map/ppermute | solution.py:31
  14.7 63.1 %collective-permute-start.1 = (f32[4,1,16,256]{3,2,1,0:T(8,128)}, f32[4,1,16,256]{3,2,1,0:T(8,128)}, u32[]{:S(2)}, u32[]{:S(2)}) collective-permute-start(f32[4,1,16,256]{3,2,1,0:T(8,128)} %get-tuple-element.58), channel_id=1, source_target_pairs={{16,0},{32,16},{48,32},{64,48},{80,64},{96,80},{112,96},{128,112},... | collective-permute-start | bytes 196616 | tf_op jit(solution)/shard_map/ppermute | solution.py:33
  27.0 66.3 %copy-start.3 = (f32[3,16,16,256]{3,1,2,0:T(8,128)}, f32[3,16,16,256]{3,1,2,0:T(8,128)S(1)}, u32[]{:S(2)}) copy-start(f32[3,16,16,256]{3,1,2,0:T(8,128)S(1)} %copy.791) | copy-start | bytes 2359300
  62.6 4.7 %copy-start.10 = (s32[2048,1]{0,1:T(1,128)S(1)}, s32[2048,1]{0,1:T(1,128)}, u32[]{:S(2)}) copy-start(s32[2048,1]{0,1:T(1,128)} %param.16) | copy-start | bytes 24580
  77.9 13.4 %copy-start.13 = (f32[17]{0:T(128)}, f32[17]{0:T(128)S(1)}, u32[]{:S(2)}) copy-start(f32[17]{0:T(128)S(1)} %and_convert_fusion) | copy-start | bytes 208
  79.0 10.6 %collective-permute-start.2 = (f32[4,18,1,256]{3,0,2,1:T(4,128)S(1)}, f32[4,18,1,256]{3,0,2,1:T(4,128)S(1)}, u32[]{:S(2)}, u32[]{:S(2)}) collective-permute-start(f32[4,18,1,256]{3,0,2,1:T(4,128)S(1)} %copy.846), channel_id=1, source_target_pairs={{0,2},{2,4},{4,6},{6,8},{8,10},{10,12},{12,14},{14,0},{1,3},{3,5},... | collective-permute-start | bytes 221192 | tf_op jit(solution)/shard_map/ppermute | solution.py:31
  83.7 7.5 %collective-permute-start.3 = (f32[4,18,1,256]{3,0,2,1:T(4,128)S(1)}, f32[4,18,1,256]{3,0,2,1:T(4,128)S(1)}, u32[]{:S(2)}, u32[]{:S(2)}) collective-permute-start(f32[4,18,1,256]{3,0,2,1:T(4,128)S(1)} %copy.847), channel_id=1, source_target_pairs={{2,0},{4,2},{6,4},{8,6},{10,8},{12,10},{14,12},{0,14},{3,1},{5,3},... | collective-permute-start | bytes 221192 | tf_op jit(solution)/shard_map/ppermute | solution.py:33
  95.4 2.7 copy-start.6
  96.1 29.2 %collective-permute-start.4 = (f32[5,16,16]{2,0,1:T(8,128)}, f32[5,16,16]{2,0,1:T(8,128)}, u32[]{:S(2)}, u32[]{:S(2)}) collective-permute-start(f32[5,16,16]{2,0,1:T(8,128)} %bitcast_select_fusion.5), channel_id=1, source_target_pairs={{0,1},{1,0},{2,3},{3,2},{4,5},{5,4},{6,7},{7,6},{8,9},{9,8},{10,11... | collective-permute-start | bytes 15368 | tf_op jit(solution)/shard_map/ppermute | solution.py:21
  106.4 1.9 copy-start.8
  106.4 1.9 copy-start.9
  117.6 161.1 %all-to-all-start = ((f32[10,32,128]{2,0,1:T(8,128)}), f32[10,32,128]{2,0,1:T(8,128)}, u32[]{:S(2)}, u32[]{:S(2)}) async-start(f32[10,32,128]{2,0,1:T(8,128)} %copy.823), calls=%async_computation.1 | async-start | bytes 524288 | tf_op jit(solution)/shard_map/all_to_all | solution.py:163
  177.3 5.0 %copy-start.7 = (f32[5,16,16,1]{2,0,1,3:T(8,128)S(1)}, f32[5,16,16,1]{2,0,1,3:T(8,128)}, u32[]{:S(2)}) copy-start(f32[5,16,16,1]{2,0,1,3:T(8,128)} %copy-done.6) | copy-start | bytes 15364
  177.3 5.0 %copy-start.15 = (pred[16]{0:T(512)(128)(4,1)S(1)}, pred[16]{0:T(512)(128)(4,1)}, u32[]{:S(2)}) copy-start(pred[16]{0:T(512)(128)(4,1)} %compare_and_fusion.2) | copy-start | bytes 52
  179.5 8.0 %copy-start.4 = (f32[3,16,16,256]{3,1,2,0:T(8,128)S(1)}, f32[3,16,16,256]{3,1,2,0:T(8,128)}, u32[]{:S(2)}) copy-start(f32[3,16,16,256]{3,1,2,0:T(8,128)} %copy-done.3) | copy-start | bytes 2359300
  189.6 1.2 copy-start.5
  196.2 11.7 %collective-permute-start.9 = (f32[5,16,16]{2,0,1:T(8,128)S(1)}, f32[5,16,16]{2,0,1:T(8,128)S(1)}, u32[]{:S(2)}, u32[]{:S(2)}) collective-permute-start(f32[5,16,16]{2,0,1:T(8,128)S(1)} %bitcast_select_fusion.2), channel_id=1, source_target_pairs={{0,1},{1,0},{2,3},{3,2},{4,5},{5,4},{6,7},{7,6},{8,9},{9,8},{10,11... | collective-permute-start | bytes 15368 | tf_op jit(solution)/shard_map/ppermute | solution.py:21
  198.8 65.5 %collective-permute-start.5 = (f32[4,1,16,256]{3,2,1,0:T(8,128)}, f32[4,1,16,256]{3,2,1,0:T(8,128)S(1)}, u32[]{:S(2)}, u32[]{:S(2)}) collective-permute-start(f32[4,1,16,256]{3,2,1,0:T(8,128)} %get-tuple-element.53), channel_id=1, source_target_pairs={{0,16},{16,32},{32,48},{48,64},{64,80},{80,96},{96,112},{112,128},... | collective-permute-start | bytes 196616 | tf_op jit(solution)/shard_map/ppermute | solution.py:31
  201.4 62.9 %collective-permute-start.6 = (f32[4,1,16,256]{3,2,1,0:T(8,128)S(1)}, f32[4,1,16,256]{3,2,1,0:T(8,128)S(1)}, u32[]{:S(2)}, u32[]{:S(2)}) collective-permute-start(f32[4,1,16,256]{3,2,1,0:T(8,128)S(1)} %get-tuple-element.54), channel_id=1, source_target_pairs={{16,0},{32,16},{48,32},{64,48},{80,64},{96,80},{112,96},{128,112},... | collective-permute-start | bytes 196616 | tf_op jit(solution)/shard_map/ppermute | solution.py:33
  264.8 7.7 %collective-permute-start.7 = (f32[4,18,1,256]{3,0,2,1:T(4,128)S(1)}, f32[4,18,1,256]{3,0,2,1:T(4,128)S(1)}, u32[]{:S(2)}, u32[]{:S(2)}) collective-permute-start(f32[4,18,1,256]{3,0,2,1:T(4,128)S(1)} %copy.851), channel_id=1, source_target_pairs={{0,2},{2,4},{4,6},{6,8},{8,10},{10,12},{12,14},{14,0},{1,3},{3,5},... | collective-permute-start | bytes 221192 | tf_op jit(solution)/shard_map/ppermute | solution.py:31
  269.0 7.5 %collective-permute-start.8 = (f32[4,18,1,256]{3,0,2,1:T(4,128)S(1)}, f32[4,18,1,256]{3,0,2,1:T(4,128)S(1)}, u32[]{:S(2)}, u32[]{:S(2)}) collective-permute-start(f32[4,18,1,256]{3,0,2,1:T(4,128)S(1)} %copy.852), channel_id=1, source_target_pairs={{2,0},{4,2},{6,4},{8,6},{10,8},{12,10},{14,12},{0,14},{3,1},{5,3},... | collective-permute-start | bytes 221192 | tf_op jit(solution)/shard_map/ppermute | solution.py:33
  272.4 4.2 %copy-start.14 = (f32[17]{0:T(128)S(1)}, f32[17]{0:T(128)}, u32[]{:S(2)}) copy-start(f32[17]{0:T(128)} %copy-done.13) | copy-start | bytes 208
  276.9 3.7 %copy-start.1 = (bf16[128,128]{1,0:T(8,128)(2,1)S(1)}, bf16[128,128]{1,0:T(8,128)(2,1)}, u32[]{:S(2)}) copy-start(bf16[128,128]{1,0:T(8,128)(2,1)} %param.13) | copy-start | bytes 98308
Sparse Core Ops, SparseCore 0:
  26.7 35.2 reduce-scatter.1
where the time goes:
time: 289 us; the launch traced here: 287 us
  blocking collectives  99 us (34%)
  local copies, waits for them, and re-layouts  89.4 us (31%)
  starting transfers between devices  46.3 us (16%)
  other arithmetic  32.7 us (11%)
  between operations  14.8 us (5%)
  waiting for transfers between devices  4.27 us (1%)
    all_gather x2, blocking collectives, interface_ghost(): picked = lax.all_gather(across, 'pitch', axis=1, tiled=True)  99 us
    unnamed x53, local copies, waits for them, and re-layouts  24.7 us
    ppermute x4, starting transfers between devices, padded(): lax.ppermute(head, axis, [((i + 1) % count, i) for i in range(count)])  21.3 us
    gather x1, local copies, waits for them, and re-layouts, local(): jnp.take(fields.reshape(fields.shape[0], -1), tracer_cells, axis=1)  18.2 us
    ppermute x4, starting transfers between devices, padded(): lax.ppermute(tail, axis, [(i, (i + 1) % count) for i in range(count)])  15.9 us
    another operation x3, other arithmetic  9.41 us
    gather x1, local copies, waits for them, and re-layouts, local(): jnp.take(jnp.stack([speed_axial, speed_pitch]).reshape(2, plane_size), tr...  7.6 us
    scatter x1, local copies, waits for them, and re-layouts, local(): outgoing = jnp.zeros((tracer_values.shape[0], npitch * capacity), jnp.flo...  6.46 us
  transfers between devices with their start and end apart: 12, of which 2 were waited for; matrix products, arithmetic and copies ran while one was open for 39% of the time, Pallas kernels for 0%

commit v1 on v0

v1 whole, which is shorter than its diff:
```python
import functools

import jax
import jax.numpy as jnp
from jax import lax
from jax.experimental import pallas as pl
from jax.experimental.pallas import tpu as pltpu
from jax.sharding import PartitionSpec as P

TIME_STEP = 0.9
AXIAL_SPEED = 0.15
PITCH_SPEED = 0.15
CHUNK = 256
MESH = pl.DeviceIdType.MESH
F32 = jnp.float32
BF16 = jnp.bfloat16


def iota(shape, dim):
    return lax.broadcasted_iota(jnp.int32, shape, dim)


def halves(x):
    high = x.astype(BF16)
    return high, (x - high.astype(F32)).astype(BF16)


def dot(a, b):
    return jnp.dot(a, b, preferred_element_type=F32)


def dot_nt(a, b):
    return lax.dot_general(a, b, (((1,), (1,)), ((), ())), preferred_element_type=F32)


def kernel(
    npitch,
    nspan,
    fields_hbm,
    kappa_hbm,
    flow_hbm,
    radial_hbm,
    values_hbm,
    cells_hbm,
    dest_hbm,
    map_ref,
    advected_ref,
    arrived_ref,
    state,
    flow_raw,
    radial,
    values,
    cells,
    dest,
    flow_own,
    flows,
    state2,
    span_send,
    span_recv,
    plane_send,
    planes_first,
    planes_second,
    speed_send,
    speed_recv,
    outgoing,
    landed,
    fparts,
    sampled,
    slots,
    counts,
    hand,
    speeds,
    coef,
    ghosts,
    load_sem,
    flow_sems,
    pitch_sems,
    span_sems,
    plane_sems,
    speed_sems,
    hand_sems,
):
    p = lax.axis_index("pitch")
    s = lax.axis_index("span")
    q = lax.axis_index("row")
    other = 1 - q
    cp, cr, ca = 16, 16, 256
    tracers = values.shape[1]
    nchunk = tracers // CHUNK

    loads = [
        pltpu.make_async_copy(flow_hbm, flow_raw, load_sem.at[0]),
        pltpu.make_async_copy(dest_hbm, dest, load_sem.at[1]),
        pltpu.make_async_copy(fields_hbm, state.at[0:3, 1 : cp + 1], load_sem.at[2]),
        pltpu.make_async_copy(kappa_hbm, state.at[3, 1 : cp + 1], load_sem.at[3]),
        pltpu.make_async_copy(cells_hbm, cells, load_sem.at[4]),
        pltpu.make_async_copy(radial_hbm, radial, load_sem.at[5]),
        pltpu.make_async_copy(values_hbm, values, load_sem.at[6]),
    ]
    for copy in loads:
        copy.start()

    def wrap(index, count):
        return lax.rem(index, count)

    barrier = pltpu.get_barrier_semaphore()

    @pl.loop(1, npitch)
    def _(step):
        pl.semaphore_signal(barrier, inc=1, device_id=(wrap(p + step, npitch), s, q), device_id_type=MESH)

    @pl.loop(0, npitch)
    def _(step):
        pl.semaphore_signal(barrier, inc=1, device_id=(wrap(p + step, npitch), s, other), device_id_type=MESH)

    @pl.loop(1, nspan)
    def _(step):
        pl.semaphore_signal(barrier, inc=1, device_id=(p, wrap(s + step, nspan), q), device_id_type=MESH)

    loads[0].wait()
    raw = flow_raw[...].astype(F32)
    flow_own[...] = jnp.concatenate([raw[:, 0, :], raw[:, 1, :]], axis=1).astype(BF16)

    lane = iota((8, 128), 1)
    source_lane = 127 * other
    near = lax.rem(lane + 128 - source_lane, 128)
    offset = pl.multiple_of(other * 128, 128)

    def pack(tiles):
        def body(i, packed):
            packed = pltpu.roll(packed, 127, 1)
            for f in range(4):
                for half in range(2):
                    group = f * 2 + half
                    tile = tiles(f, i, half)
                    spot = group * 16 + 15
                    packed = jnp.where(near == spot, pltpu.roll(tile, spot, 1), packed)
            return packed

        packed = lax.fori_loop(0, cp, body, jnp.zeros((8, 128), F32))
        return jnp.where(q == 0, pltpu.roll(packed, 1, 1), packed)

    loads[2].wait()
    loads[3].wait()
    plane_send[0] = pack(lambda f, i, half: state[f, i + 1, pl.ds(half * 8, 8), pl.ds(offset, 128)])

    @pl.loop(0, cp)
    def _(i):
        for f in range(4):
            span_send[0, 0, f, pl.ds(i, 1), :] = state[f, i + 1, 0:1, :]
            span_send[0, 1, f, pl.ds(i, 1), :] = state[f, i + 1, cr - 1 : cr, :]

    pl.semaphore_wait(barrier, 2 * npitch - 1 + nspan - 1)

    @pl.loop(1, nspan)
    def _(step):
        pltpu.make_async_remote_copy(
            src_ref=flow_own,
            dst_ref=flows.at[s],
            send_sem=flow_sems.at[0],
            recv_sem=flow_sems.at[1],
            device_id=(p, wrap(s + step, nspan), q),
            device_id_type=MESH,
        ).start()

    flows[s] = flow_own[...]

    up, down = wrap(p + 1, npitch), wrap(p + npitch - 1, npitch)
    outer, inner = wrap(s + 1, nspan), wrap(s + nspan - 1, nspan)

    def halo(ref, step, count):
        return [
            pltpu.make_async_remote_copy(
                src_ref=ref.at[0:count, cp],
                dst_ref=ref.at[0:count, 0],
                send_sem=pitch_sems.at[step, 0],
                recv_sem=pitch_sems.at[step, 1],
                device_id=(up, s, q),
                device_id_type=MESH,
            ),
            pltpu.make_async_remote_copy(
                src_ref=ref.at[0:count, 1],
                dst_ref=ref.at[0:count, cp + 1],
                send_sem=pitch_sems.at[step, 2],
                recv_sem=pitch_sems.at[step, 3],
                device_id=(down, s, q),
                device_id_type=MESH,
            ),
            pltpu.make_async_remote_copy(
                src_ref=span_send.at[step, 0, 0:count],
                dst_ref=span_recv.at[step, 1, 0:count],
                send_sem=span_sems.at[step, 0],
                recv_sem=span_sems.at[step, 1],
                device_id=(p, inner, q),
                device_id_type=MESH,
            ),
            pltpu.make_async_remote_copy(
                src_ref=span_send.at[step, 1, 0:count],
                dst_ref=span_recv.at[step, 0, 0:count],
                send_sem=span_sems.at[step, 2],
                recv_sem=span_sems.at[step, 3],
                device_id=(p, outer, q),
                device_id_type=MESH,
            ),
        ]

    planes = (planes_first, planes_second)

    def spread_plane(step):
        @pl.loop(0, npitch)
        def _(far):
            pltpu.make_async_remote_copy(
                src_ref=plane_send.at[step],
                dst_ref=planes[step].at[p],
                send_sem=plane_sems.at[step, 0],
                recv_sem=plane_sems.at[step, 1],
                device_id=(wrap(p + far, npitch), s, other),
                device_id_type=MESH,
            ).start()

    def wait_plane(step):
        pltpu.make_async_copy(planes[step], planes[step], plane_sems.at[step, 0]).wait()
        pltpu.make_async_copy(planes[step], planes[step], plane_sems.at[step, 1]).wait()

    first = halo(state, 0, 4)
    for copy in first:
        copy.start()
    spread_plane(0)

    for f in range(3):
        block = state[f, 1 : cp + 1].reshape(cp * cr, ca)
        high, low = halves(block)
        fparts[0, f] = high
        fparts[1, f] = low
    loads[1].wait()
    loads[4].wait()
    counts[...] = jnp.zeros((npitch, 1), F32)
    before = (iota((CHUNK, CHUNK), 0) < iota((CHUNK, CHUNK), 1)).astype(F32).astype(BF16)

    @pl.loop(0, nchunk)
    def _(chunk):
        here = pl.ds(pl.multiple_of(chunk * CHUNK, CHUNK), CHUNK)
        cell = cells[0:1, here]
        axial = lax.bitwise_and(cell, ca - 1)
        place = lax.shift_right_logical(cell, 8)
        onehot = (iota((ca, CHUNK), 0) == axial).astype(F32).astype(BF16)
        at_place = iota((cp * cr, CHUNK), 0) == place
        for f in range(3):
            picked = dot(fparts[0, f], onehot) + dot(fparts[1, f], onehot)
            sampled[f : f + 1, here] = jnp.sum(jnp.where(at_place, picked, 0.0), axis=0, keepdims=True)
        goal = dest[0:1, here]
        mine = iota((npitch, CHUNK), 0) == goal
        mine_f = mine.astype(F32)
        rank = dot(mine_f.astype(BF16), before) + counts[...]
        slots[0:1, here] = jnp.sum(jnp.where(mine, rank, 0.0), axis=0, keepdims=True)
        counts[...] += jnp.sum(mine_f, axis=1, keepdims=True)

    some = flows.at[0 : nspan - 1]
    pltpu.make_async_copy(some, some, flow_sems.at[0]).wait()
    pltpu.make_async_copy(some, some, flow_sems.at[1]).wait()

    loads[5].wait()
    kernel_rows = radial[pl.ds(pl.multiple_of(s * cr, cr), cr), :]
    smoothed = dot(kernel_rows, flows[...].reshape(nspan * cr, 2 * ca))
    speed_axial = AXIAL_SPEED * (1.0 + 0.5 * jnp.tanh(smoothed[:, :ca]))
    speed_pitch = PITCH_SPEED * jnp.tanh(smoothed[:, ca:])
    speeds[0] = speed_axial
    speeds[1] = speed_pitch
    edge = jnp.where(q == 0, speed_axial[:, ca - 1 : ca], speed_axial[:, 0:1])
    speed_send[...] = jnp.broadcast_to(edge, (cr, 128))
    speed_copy = pltpu.make_async_remote_copy(
        src_ref=speed_send,
        dst_ref=speed_recv,
        send_sem=speed_sems.at[0],
        recv_sem=speed_sems.at[1],
        device_id=(p, s, other),
        device_id_type=MESH,
    )
    speed_copy.start()

    loads[6].wait()
    hand[...] = jnp.zeros(hand.shape, F32)
    speed_parts = halves(speeds[...].reshape(2 * cr, ca))

    @pl.loop(0, nchunk)
    def _(chunk):
        here = pl.ds(pl.multiple_of(chunk * CHUNK, CHUNK), CHUNK)
        cell = cells[0:1, here]
        axial = lax.bitwise_and(cell, ca - 1)
        onehot = (iota((ca, CHUNK), 0) == axial).astype(F32).astype(BF16)
        picked = dot(speed_parts[0], onehot) + dot(speed_parts[1], onehot)
        radius = lax.bitwise_and(lax.shift_right_logical(cell, 8), cr - 1)
        at_radius = iota((cr, CHUNK), 0) == radius
        got = [sampled[f : f + 1, here] for f in range(3)]
        for k in range(2):
            got.append(jnp.sum(jnp.where(at_radius, picked[k * cr : (k + 1) * cr], 0.0), axis=0, keepdims=True))
        which = iota((16, CHUNK), 0)
        item = jnp.where(which >= 5, which - 5, which)
        samples = jnp.zeros((16, CHUNK), F32)
        for k in range(5):
            samples = jnp.where(item == k, got[k], samples)
        old = jnp.concatenate([values[:, here], jnp.zeros((6, CHUNK), F32)], axis=0)
        updated = jnp.where(which < 5, old + 0.5 * (samples - old), old + 0.8 * samples)
        high, low = halves(updated)
        slot = slots[0:1, here].astype(jnp.int32)
        slot_hot = (iota((128, CHUNK), 0) == slot).astype(F32).astype(BF16)
        goal = jnp.broadcast_to(dest[0:1, here], (16, CHUNK))
        zero = jnp.zeros((16, CHUNK), F32)
        masks = [goal == d for d in range(npitch)]
        left = jnp.concatenate([jnp.where(m, high.astype(F32), zero).astype(BF16) for m in masks], axis=0)
        hand[...] += dot_nt(left, slot_hot)
        left = jnp.concatenate([jnp.where(m, low.astype(F32), zero).astype(BF16) for m in masks], axis=0)
        hand[...] += dot_nt(left, slot_hot)

    for d in range(npitch):
        outgoing[d] = hand[d * 16 : d * 16 + 10, :]

    @pl.loop(1, npitch)
    def _(step):
        to = wrap(p + step, npitch)
        pltpu.make_async_remote_copy(
            src_ref=outgoing.at[to],
            dst_ref=landed.at[p],
            send_sem=hand_sems.at[0],
            recv_sem=hand_sems.at[1],
            device_id=(to, s, q),
            device_id_type=MESH,
        ).start()

    landed[p] = outgoing[p]

    for copy in first:
        copy.wait()
    wait_plane(0)
    speed_copy.wait()

    start_cell = map_ref[0, 0]
    facing = lax.shift_right_logical(start_cell, 4)
    shift = lax.bitwise_and(start_cell, 15)
    facing_next = lax.bitwise_and(facing + 1, npitch - 1)
    in_group = lax.bitwise_and(lane, 15)

    def ghost(step, count):
        low = planes[step][facing]
        high = planes[step][facing_next]
        high = pltpu.roll(high, 16, 1)
        for bit in range(4):
            moved = lax.bitwise_and(shift, 1 << bit) != 0
            low = jnp.where(moved, pltpu.roll(low, 128 - (1 << bit), 1), low)
            high = jnp.where(moved, pltpu.roll(high, 128 - (1 << bit), 1), high)
        window = jnp.where(in_group + shift < 16, low, high)

        def body(i, tile):
            for f in range(count):
                for half in range(2):
                    group = f * 2 + half
                    ghosts[f, i, half * 8 : half * 8 + 8, :] = jnp.broadcast_to(
                        tile[:, group * 16 : group * 16 + 1], (8, 128)
                    )
            return pltpu.roll(tile, 127, 1)

        lax.fori_loop(0, cp, body, window)

    ghost(0, 4)
    lanes = iota((cr, ca), 1)
    radii = iota((cr, ca), 0)
    west, east = lanes == 0, lanes == ca - 1
    hub, tip = radii == 0, radii == cr - 1
    stator = q == 0
    span_first = s == 0
    span_last = s == nspan - 1

    def twice(x):
        return jnp.concatenate([x, x], axis=1)

    def around(x, inner_row, outer_row, ghost_tile):
        out = jnp.where(tip, outer_row, pltpu.roll(x, cr - 1, 0))
        inn = jnp.where(hub, inner_row, pltpu.roll(x, 1, 0))
        right = jnp.where(east, ghost_tile, pltpu.roll(x, ca - 1, 1))
        left = jnp.where(west, ghost_tile, pltpu.roll(x, 1, 1))
        return out, inn, right, left

    sa = speeds[0]
    sp = speeds[1]
    ghost_speed = twice(speed_recv[...])
    no_west = jnp.logical_and(west, stator)
    no_east = jnp.logical_and(east, jnp.logical_not(stator))
    sa_right = jnp.where(no_east, sa, jnp.where(east, ghost_speed, pltpu.roll(sa, ca - 1, 1)))
    sa_left = jnp.where(no_west, sa, jnp.where(west, ghost_speed, pltpu.roll(sa, 1, 1)))
    w_east = 0.5 * (sa + sa_right)
    w_west = 0.5 * (sa + sa_left)
    ep, em = jnp.maximum(w_east, 0.0), jnp.minimum(w_east, 0.0)
    wp, wm = jnp.maximum(w_west, 0.0), jnp.minimum(w_west, 0.0)
    pp, pm = jnp.maximum(sp, 0.0), jnp.minimum(sp, 0.0)
    no_inner = jnp.logical_and(hub, span_first)
    no_outer = jnp.logical_and(tip, span_last)

    @pl.loop(0, cp)
    def _(i):
        k = state[3, i + 1]
        k_out, k_in, k_right, k_left = around(
            k, span_recv[0, 0, 3, pl.ds(i, 1), :], span_recv[0, 1, 3, pl.ds(i, 1), :], twice(ghosts[3, i])
        )
        k_right = jnp.where(no_east, k, k_right)
        k_left = jnp.where(no_west, k, k_left)
        d_up = 0.5 * (k + state[3, i + 2])
        d_down = 0.5 * (k + state[3, i])
        d_out = jnp.where(no_outer, 0.0, 0.5 * (k + k_out))
        d_in = jnp.where(no_inner, 0.0, 0.5 * (k + k_in))
        d_east = 0.5 * (k + k_right)
        d_west = 0.5 * (k + k_left)
        c_up = TIME_STEP * (d_up - pm)
        c_down = TIME_STEP * (d_down + pp)
        c_out = TIME_STEP * d_out
        c_in = TIME_STEP * d_in
        c_east = TIME_STEP * (d_east - em)
        c_west = TIME_STEP * (d_west + wp)
        center = 1.0 - (c_up + c_down + c_out + c_in) - TIME_STEP * (ep + d_east + d_west - wm)
        center = center + jnp.where(no_east, c_east, 0.0) + jnp.where(no_west, c_west, 0.0)
        coef[0, i] = center
        coef[1, i] = c_up
        coef[2, i] = c_down
        coef[3, i] = c_out
        coef[4, i] = c_in
        coef[5, i] = jnp.where(no_east, 0.0, c_east)
        coef[6, i] = jnp.where(no_west, 0.0, c_west)

    def advance(old, step, store):
        @pl.loop(0, cp)
        def _(i):
            c = [coef[n, i] for n in range(7)]
            for f in range(3):
                v = old[f, i + 1]
                out, inn, right, left = around(
                    v, span_recv[step, 0, f, pl.ds(i, 1), :], span_recv[step, 1, f, pl.ds(i, 1), :], twice(ghosts[f, i])
                )
                new = c[0] * v + c[1] * old[f, i + 2] + c[2] * old[f, i]
                new = new + c[3] * out + c[4] * inn + c[5] * right + c[6] * left
                store(f, i, new)

    def store_first(f, i, new):
        state2[f, i + 1] = new
        span_send[1, 0, f, pl.ds(i, 1), :] = new[0:1, :]
        span_send[1, 1, f, pl.ds(i, 1), :] = new[cr - 1 : cr, :]

    advance(state, 0, store_first)

    second = halo(state2, 1, 3)
    for copy in second:
        copy.start()
    plane_send[1] = pack(lambda f, i, half: state2[min(f, 2), i + 1, pl.ds(half * 8, 8), pl.ds(offset, 128)])
    spread_plane(1)
    for copy in second:
        copy.wait()
    wait_plane(1)
    ghost(1, 3)

    def store_second(f, i, new):
        advected_ref[f, i] = new

    advance(state2, 1, store_second)

    many = landed.at[0 : npitch - 1]
    pltpu.make_async_copy(many, many, hand_sems.at[0]).wait()
    pltpu.make_async_copy(many, many, hand_sems.at[1]).wait()

    for d in range(npitch):
        arrived_ref[:, d * 128 : (d + 1) * 128] = landed[d]


def local(fields, diffusivity, mean_flow, radial_kernel, tracer_values, tracer_cells, tracer_dest, interface_map):
    npitch = lax.axis_size("pitch")
    nspan = lax.axis_size("span")
    tracers = tracer_values.shape[1]
    anywhere = pl.BlockSpec(memory_space=pltpu.HBM)
    vmem = pl.BlockSpec(memory_space=pltpu.VMEM)
    dma = pltpu.SemaphoreType.DMA
    return pl.pallas_call(
        functools.partial(kernel, npitch, nspan),
        out_shape=(
            jax.ShapeDtypeStruct((3, 16, 16, 256), F32),
            jax.ShapeDtypeStruct((10, npitch * 128), F32),
        ),
        in_specs=[anywhere] * 7 + [pl.BlockSpec(memory_space=pltpu.SMEM)],
        out_specs=(vmem, vmem),
        scratch_shapes=[
            pltpu.VMEM((4, 18, 16, 256), F32),
            pltpu.VMEM((16, 2, 256), BF16),
            pltpu.VMEM((128, nspan * 16), BF16),
            pltpu.VMEM((10, tracers), F32),
            pltpu.VMEM((1, tracers), jnp.int32),
            pltpu.VMEM((1, tracers), jnp.int32),
            pltpu.VMEM((16, 512), BF16),
            pltpu.VMEM((nspan, 16, 512), BF16),
            pltpu.VMEM((3, 18, 16, 256), F32),
            pltpu.VMEM((2, 2, 4, 16, 256), F32),
            pltpu.VMEM((2, 2, 4, 16, 256), F32),
            pltpu.VMEM((2, 8, 128), F32),
            pltpu.VMEM((npitch, 8, 128), F32),
            pltpu.VMEM((npitch, 8, 128), F32),
            pltpu.VMEM((16, 128), F32),
            pltpu.VMEM((16, 128), F32),
            pltpu.VMEM((npitch, 10, 128), F32),
            pltpu.VMEM((npitch, 10, 128), F32),
            pltpu.VMEM((2, 3, 256, 256), BF16),
            pltpu.VMEM((8, tracers), F32),
            pltpu.VMEM((8, tracers), F32),
            pltpu.VMEM((npitch, 1), F32),
            pltpu.VMEM((npitch * 16, 128), F32),
            pltpu.VMEM((2, 16, 256), F32),
            pltpu.VMEM((7, 16, 16, 256), F32),
            pltpu.VMEM((4, 16, 16, 128), F32),
            dma((7,)),
            dma((2,)),
            dma((2, 4)),
            dma((2, 4)),
            dma((2, 2)),
            dma((2,)),
            dma((2,)),
        ],
        compiler_params=pltpu.CompilerParams(
            collective_id=0, has_side_effects=True, vmem_limit_bytes=60 * 1024 * 1024
        ),
        name="row_step",
    )(
        fields,
        diffusivity,
        mean_flow,
        radial_kernel,
        tracer_values,
        tracer_cells.reshape(1, tracers),
        tracer_dest.reshape(1, tracers),
        interface_map,
    )


def solution(mesh):
    placed = (
        P(None, "pitch", "span", "row"),
        P("pitch", "span", "row"),
        P("span", None, "row"),
        P(),
        P(None, ("pitch", "span", "row")),
        P(("pitch", "span", "row")),
        P(("pitch", "span", "row"), None),
        P("row", "pitch"),
    )
    return jax.shard_map(
        local,
        mesh=mesh,
        in_specs=placed,
        out_specs=(P(None, "pitch", "span", "row"), P(None, ("pitch", "span", "row"))),
        check_vma=False,
    )
```

time: 289 us -> 49.9 us (0.17)
  the two profiles are of different devices: /device:TPU:24 before, /device:TPU:1 now
where the time goes in v1:
time: 49.9 us; the launch traced here: 49.7 us
  Pallas kernels  46.2 us (93%)
  local copies, waits for them, and re-layouts  2.81 us (6%)
  between operations  0.65 us (1%)
    pallas_call x1, Pallas kernels, local(): pl.pallas_call(functools.partial(kernel, npitch, nspan), out_shape=(jax.S...  46.2 us
    unnamed x4, local copies, waits for them, and re-layouts  2.81 us

profile of v1, /device:TPU:1, one launch (start us, length us, event | category | flops | bytes accessed | tf_op | source)
XLA Modules:
  0.0 49.7 jit_solution(9362794320697297699)
XLA Ops:
  0.6 46.2 %row_step.1 = (f32[3,16,16,256]{3,2,1,0:T(8,128)}, f32[10,4096]{1,0:T(8,128)}) custom-call(f32[3,16,16,256]{3,2,1,0:T(8,128)} %fields_hbm.1, f32[16,16,256]{2,1,0:T(8,128)} %kappa_hbm.1, bf16[16,2,256]{2,1,0:T(2,128)(2,1)} %flow_hbm.1, bf16[128,128]{1,0:T(8,128)(2,1)} %radial_hbm.1, f32[10,2048]{1,0:T(8,128)} %values_hbm.1, s32[1,2048]{1,0:T(1,128)} %bitcast.2, ...), custom_call_target="tpu_custom_call" | custom-call | tf_op jit(solution)/shard_map/row_step/pallas_call | solution.py:478
  46.9 0.0 copy-start
  46.9 2.1 %copy.12 = f32[3,16,16,256]{3,2,1,0:T(8,128)} copy(f32[3,16,16,256]{3,2,1,0:T(8,128)} %get-tuple-element.4) | data formatting | bytes 1572864
  49.0 0.0 copy-done
  49.0 0.7 %copy.13 = f32[10,4096]{1,0:T(8,128)} copy(f32[10,4096]{1,0:T(8,128)S(1)} %copy-done) | data formatting | bytes 327680
Async XLA Ops:
  46.9 2.1 %copy-start = (f32[10,4096]{1,0:T(8,128)S(1)}, f32[10,4096]{1,0:T(8,128)}, u32[]{:S(2)}) copy-start(f32[10,4096]{1,0:T(8,128)} %get-tuple-element.5) | copy-start | bytes 491524

commit v2 on v1

--- a/solution.py
+++ b/solution.py
@@ -10,7 +10,9 @@
 TIME_STEP = 0.9
 AXIAL_SPEED = 0.15
 PITCH_SPEED = 0.15
-CHUNK = 256
+CHUNK = 512
+UNROLL = 16
+DEEP = 8
 MESH = pl.DeviceIdType.MESH
 F32 = jnp.float32
 BF16 = jnp.bfloat16
@@ -58,11 +60,13 @@
     span_send,
     span_recv,
     plane_send,
+    plane_in,
     planes_first,
     planes_second,
     speed_send,
     speed_recv,
     outgoing,
+    midway,
     landed,
     fparts,
     sampled,
@@ -101,48 +105,103 @@
         copy.start()
 
     def wrap(index, count):
-        return lax.rem(index, count)
+        return lax.bitwise_and(index, count - 1)
 
     barrier = pltpu.get_barrier_semaphore()
 
-    @pl.loop(1, npitch)
-    def _(step):
-        pl.semaphore_signal(barrier, inc=1, device_id=(wrap(p + step, npitch), s, q), device_id_type=MESH)
-
-    @pl.loop(0, npitch)
-    def _(step):
-        pl.semaphore_signal(barrier, inc=1, device_id=(wrap(p + step, npitch), s, other), device_id_type=MESH)
-
-    @pl.loop(1, nspan)
-    def _(step):
-        pl.semaphore_signal(barrier, inc=1, device_id=(p, wrap(s + step, nspan), q), device_id_type=MESH)
+    wide = npitch // DEEP
+    x, z = lax.shift_right_logical(p, 3), lax.bitwise_and(p, DEEP - 1)
+    z_peers = [x * DEEP + wrap(z + step, DEEP) for step in range(1, DEEP)]
+    x_peers = [wrap(p + step * DEEP, npitch) for step in range(1, wide)]
+    span_peers = [wrap(s + step, nspan) for step in range(1, nspan)]
+    up, down = wrap(p + 1, npitch), wrap(p + npitch - 1, npitch)
+    outer, inner = wrap(s + 1, nspan), wrap(s + nspan - 1, nspan)
+    greeted = [(p, s, other), (up, s, q), (down, s, q)]
+    greeted += [(p, peer, q) for peer in span_peers]
+    greeted += [(peer, s, q) for peer in z_peers + x_peers]
+    for device in greeted:
+        pl.semaphore_signal(barrier, inc=1, device_id=device, device_id_type=MESH)
 
     loads[0].wait()
     raw = flow_raw[...].astype(F32)
     flow_own[...] = jnp.concatenate([raw[:, 0, :], raw[:, 1, :]], axis=1).astype(BF16)
 
+    pl.semaphore_wait(barrier, len(greeted))
+
+    def send(src, dst, sems, first, device):
+        return pltpu.make_async_remote_copy(
+            src_ref=src,
+            dst_ref=dst,
+            send_sem=sems.at[first],
+            recv_sem=sems.at[first + 1],
+            device_id=device,
+            device_id_type=MESH,
+        )
+
+    def drain(ref, sems, first):
+        pltpu.make_async_copy(ref, ref, sems.at[first]).wait()
+        pltpu.make_async_copy(ref, ref, sems.at[first + 1]).wait()
+
+    for peer in span_peers:
+        send(flow_own, flows.at[s], flow_sems, 0, (p, peer, q)).start()
+
+    flows[s] = flow_own[...]
+
     lane = iota((8, 128), 1)
     source_lane = 127 * other
-    near = lax.rem(lane + 128 - source_lane, 128)
+    near = lax.bitwise_and(lane + 128 - source_lane, 127)
     offset = pl.multiple_of(other * 128, 128)
 
-    def pack(tiles):
-        def body(i, packed):
-            packed = pltpu.roll(packed, 127, 1)
-            for f in range(4):
-                for half in range(2):
-                    group = f * 2 + half
+    def pack(fields, tiles):
+        parts = []
+        for f in range(fields):
+            for half in range(2):
+                part = jnp.zeros((8, 128), F32)
+                for i in range(cp):
+                    spot = (f * 2 + half) * 16 + i
                     tile = tiles(f, i, half)
-                    spot = group * 16 + 15
-                    packed = jnp.where(near == spot, pltpu.roll(tile, spot, 1), packed)
-            return packed
-
-        packed = lax.fori_loop(0, cp, body, jnp.zeros((8, 128), F32))
-        return jnp.where(q == 0, pltpu.roll(packed, 1, 1), packed)
+                    part = jnp.where(near == spot, pltpu.roll(tile, spot, 1) if spot else tile, part)
+                parts.append(part)
+        while len(parts) > 1:
+            parts = [sum(parts[n : n + 2]) for n in range(0, len(parts), 2)]
+        return jnp.where(q == 0, pltpu.roll(parts[0], 1, 1), parts[0])
+
+    def halo(ref, step, count):
+        pitch, span = pitch_sems.at[step], span_sems.at[step]
+        return [
+            send(ref.at[0:count, cp], ref.at[0:count, 0], pitch, 0, (up, s, q)),
+            send(ref.at[0:count, 1], ref.at[0:count, cp + 1], pitch, 2, (down, s, q)),
+            send(span_send.at[step, 0, 0:count], span_recv.at[step, 1, 0:count], span, 0, (p, inner, q)),
+            send(span_send.at[step, 1, 0:count], span_recv.at[step, 0, 0:count], span, 2, (p, outer, q)),
+        ]
+
+    planes = (planes_first, planes_second)
+
+    def swap_plane(step):
+        return send(plane_send.at[step], plane_in.at[step], plane_sems.at[step], 0, (p, s, other))
+
+    def spread_z(step):
+        for peer in z_peers:
+            send(plane_in.at[step], planes[step].at[x, z], plane_sems.at[step], 2, (peer, s, q)).start()
+        planes[step][x, z] = plane_in[step]
+
+    def spread_x(step):
+        drain(planes[step].at[0, 0 : DEEP - 1], plane_sems.at[step], 2)
+        for peer in x_peers:
+            send(planes[step].at[x], planes[step].at[x], plane_sems.at[step], 4, (peer, s, q)).start()
+
+    def wait_plane(step):
+        drain(planes[step].at[0 : wide - 1], plane_sems.at[step], 4)
 
     loads[2].wait()
     loads[3].wait()
-    plane_send[0] = pack(lambda f, i, half: state[f, i + 1, pl.ds(half * 8, 8), pl.ds(offset, 128)])
+    plane_send[0] = pack(4, lambda f, i, half: state[f, i + 1, pl.ds(half * 8, 8), pl.ds(offset, 128)])
+
+    swap = swap_plane(0)
+    swap.start()
+    first = halo(state, 0, 4)
+    for copy in first[:2]:
+        copy.start()
 
     @pl.loop(0, cp)
     def _(i):
@@ -150,82 +209,8 @@
             span_send[0, 0, f, pl.ds(i, 1), :] = state[f, i + 1, 0:1, :]
             span_send[0, 1, f, pl.ds(i, 1), :] = state[f, i + 1, cr - 1 : cr, :]
 
-    pl.semaphore_wait(barrier, 2 * npitch - 1 + nspan - 1)
-
-    @pl.loop(1, nspan)
-    def _(step):
-        pltpu.make_async_remote_copy(
-            src_ref=flow_own,
-            dst_ref=flows.at[s],
-            send_sem=flow_sems.at[0],
-            recv_sem=flow_sems.at[1],
-            device_id=(p, wrap(s + step, nspan), q),
-            device_id_type=MESH,
-        ).start()
-
-    flows[s] = flow_own[...]
-
-    up, down = wrap(p + 1, npitch), wrap(p + npitch - 1, npitch)
-    outer, inner = wrap(s + 1, nspan), wrap(s + nspan - 1, nspan)
-
-    def halo(ref, step, count):
-        return [
-            pltpu.make_async_remote_copy(
-                src_ref=ref.at[0:count, cp],
-                dst_ref=ref.at[0:count, 0],
-                send_sem=pitch_sems.at[step, 0],
-                recv_sem=pitch_sems.at[step, 1],
-                device_id=(up, s, q),
-                device_id_type=MESH,
-            ),
-            pltpu.make_async_remote_copy(
-                src_ref=ref.at[0:count, 1],
-                dst_ref=ref.at[0:count, cp + 1],
-                send_sem=pitch_sems.at[step, 2],
-                recv_sem=pitch_sems.at[step, 3],
-                device_id=(down, s, q),
-                device_id_type=MESH,
-            ),
-            pltpu.make_async_remote_copy(
-                src_ref=span_send.at[step, 0, 0:count],
-                dst_ref=span_recv.at[step, 1, 0:count],
-                send_sem=span_sems.at[step, 0],
-                recv_sem=span_sems.at[step, 1],
-                device_id=(p, inner, q),
-                device_id_type=MESH,
-            ),
-            pltpu.make_async_remote_copy(
-                src_ref=span_send.at[step, 1, 0:count],
-                dst_ref=span_recv.at[step, 0, 0:count],
-                send_sem=span_sems.at[step, 2],
-                recv_sem=span_sems.at[step, 3],
-                device_id=(p, outer, q),
-                device_id_type=MESH,
-            ),
-        ]
-
-    planes = (planes_first, planes_second)
-
-    def spread_plane(step):
-        @pl.loop(0, npitch)
-        def _(far):
-            pltpu.make_async_remote_copy(
-                src_ref=plane_send.at[step],
-                dst_ref=planes[step].at[p],
-                send_sem=plane_sems.at[step, 0],
-                recv_sem=plane_sems.at[step, 1],
-                device_id=(wrap(p + far, npitch), s, other),
-                device_id_type=MESH,
-            ).start()
-
-    def wait_plane(step):
-        pltpu.make_async_copy(planes[step], planes[step], plane_sems.at[step, 0]).wait()
-        pltpu.make_async_copy(planes[step], planes[step], plane_sems.at[step, 1]).wait()
-
-    first = halo(state, 0, 4)
-    for copy in first:
+    for copy in first[2:]:
         copy.start()
-    spread_plane(0)
 
     for f in range(3):
         block = state[f, 1 : cp + 1].reshape(cp * cr, ca)
@@ -234,16 +219,17 @@
         fparts[1, f] = low
     loads[1].wait()
     loads[4].wait()
+    numbers = iota((256, CHUNK), 0).astype(F32).astype(BF16)
+    one, zero = jnp.asarray(1, BF16), jnp.asarray(0, BF16)
     counts[...] = jnp.zeros((npitch, 1), F32)
     before = (iota((CHUNK, CHUNK), 0) < iota((CHUNK, CHUNK), 1)).astype(F32).astype(BF16)
 
-    @pl.loop(0, nchunk)
-    def _(chunk):
-        here = pl.ds(pl.multiple_of(chunk * CHUNK, CHUNK), CHUNK)
+    def sample(chunk):
+        here = pl.ds(chunk * CHUNK, CHUNK)
         cell = cells[0:1, here]
         axial = lax.bitwise_and(cell, ca - 1)
         place = lax.shift_right_logical(cell, 8)
-        onehot = (iota((ca, CHUNK), 0) == axial).astype(F32).astype(BF16)
+        onehot = jnp.where(numbers == axial.astype(F32).astype(BF16), one, zero)
         at_place = iota((cp * cr, CHUNK), 0) == place
         for f in range(3):
             picked = dot(fparts[0, f], onehot) + dot(fparts[1, f], onehot)
@@ -255,6 +241,13 @@
         slots[0:1, here] = jnp.sum(jnp.where(mine, rank, 0.0), axis=0, keepdims=True)
         counts[...] += jnp.sum(mine_f, axis=1, keepdims=True)
 
+    sample(0)
+    swap.wait()
+    spread_z(0)
+    sample(1)
+    spread_x(0)
+    sample(2)
+
     some = flows.at[0 : nspan - 1]
     pltpu.make_async_copy(some, some, flow_sems.at[0]).wait()
     pltpu.make_async_copy(some, some, flow_sems.at[1]).wait()
@@ -268,26 +261,19 @@
     speeds[1] = speed_pitch
     edge = jnp.where(q == 0, speed_axial[:, ca - 1 : ca], speed_axial[:, 0:1])
     speed_send[...] = jnp.broadcast_to(edge, (cr, 128))
-    speed_copy = pltpu.make_async_remote_copy(
-        src_ref=speed_send,
-        dst_ref=speed_recv,
-        send_sem=speed_sems.at[0],
-        recv_sem=speed_sems.at[1],
-        device_id=(p, s, other),
-        device_id_type=MESH,
-    )
+    speed_copy = send(speed_send, speed_recv, speed_sems, 0, (p, s, other))
     speed_copy.start()
+    sample(3)
 
     loads[6].wait()
     hand[...] = jnp.zeros(hand.shape, F32)
     speed_parts = halves(speeds[...].reshape(2 * cr, ca))
 
-    @pl.loop(0, nchunk)
-    def _(chunk):
-        here = pl.ds(pl.multiple_of(chunk * CHUNK, CHUNK), CHUNK)
+    def pass_on(chunk):
+        here = pl.ds(chunk * CHUNK, CHUNK)
         cell = cells[0:1, here]
         axial = lax.bitwise_and(cell, ca - 1)
-        onehot = (iota((ca, CHUNK), 0) == axial).astype(F32).astype(BF16)
+        onehot = jnp.where(numbers == axial.astype(F32).astype(BF16), one, zero)
         picked = dot(speed_parts[0], onehot) + dot(speed_parts[1], onehot)
         radius = lax.bitwise_and(lax.shift_right_logical(cell, 8), cr - 1)
         at_radius = iota((cr, CHUNK), 0) == radius
@@ -302,36 +288,29 @@
         old = jnp.concatenate([values[:, here], jnp.zeros((6, CHUNK), F32)], axis=0)
         updated = jnp.where(which < 5, old + 0.5 * (samples - old), old + 0.8 * samples)
         high, low = halves(updated)
-        slot = slots[0:1, here].astype(jnp.int32)
-        slot_hot = (iota((128, CHUNK), 0) == slot).astype(F32).astype(BF16)
-        goal = jnp.broadcast_to(dest[0:1, here], (16, CHUNK))
-        zero = jnp.zeros((16, CHUNK), F32)
-        masks = [goal == d for d in range(npitch)]
-        left = jnp.concatenate([jnp.where(m, high.astype(F32), zero).astype(BF16) for m in masks], axis=0)
-        hand[...] += dot_nt(left, slot_hot)
-        left = jnp.concatenate([jnp.where(m, low.astype(F32), zero).astype(BF16) for m in masks], axis=0)
-        hand[...] += dot_nt(left, slot_hot)
-
+        goal = dest[0:1, here]
+        odd = lax.bitwise_and(goal, 1).astype(F32)
+        column = (slots[0:1, here] + 128.0 * odd).astype(BF16)
+        hot = jnp.where(numbers == column, one, zero)
+        pair = jnp.broadcast_to(lax.shift_right_logical(goal, 1).astype(F32), (16, CHUNK)).astype(BF16)
+        pair = jnp.concatenate([pair, pair], axis=1)
+        both = jnp.concatenate([high, low], axis=1)
+        left = jnp.concatenate([jnp.where(pair == jnp.asarray(d, BF16), both, zero) for d in range(npitch // 2)], axis=0)
+        hand[...] += dot_nt(left, jnp.concatenate([hot, hot], axis=1))
+
+    for chunk in range(nchunk):
+        pass_on(chunk)
     for d in range(npitch):
-        outgoing[d] = hand[d * 16 : d * 16 + 10, :]
-
-    @pl.loop(1, npitch)
-    def _(step):
-        to = wrap(p + step, npitch)
-        pltpu.make_async_remote_copy(
-            src_ref=outgoing.at[to],
-            dst_ref=landed.at[p],
-            send_sem=hand_sems.at[0],
-            recv_sem=hand_sems.at[1],
-            device_id=(to, s, q),
-            device_id_type=MESH,
-        ).start()
-
-    landed[p] = outgoing[p]
-
+        row, column = d // 2 * 16, d % 2 * 128
+        outgoing[d % DEEP, d // DEEP] = hand[row : row + 10, column : column + 128]
+    for step, peer in enumerate(z_peers):
+        far = wrap(z + step + 1, DEEP)
+        send(outgoing.at[far], midway.at[z], hand_sems, 0, (peer, s, q)).start()
+    midway[z] = outgoing[z]
+
+    wait_plane(0)
     for copy in first:
         copy.wait()
-    wait_plane(0)
     speed_copy.wait()
 
     start_cell = map_ref[0, 0]
@@ -341,8 +320,8 @@
     in_group = lax.bitwise_and(lane, 15)
 
     def ghost(step, count):
-        low = planes[step][facing]
-        high = planes[step][facing_next]
+        low = planes[step][lax.shift_right_logical(facing, 3), lax.bitwise_and(facing, DEEP - 1)]
+        high = planes[step][lax.shift_right_logical(facing_next, 3), lax.bitwise_and(facing_next, DEEP - 1)]
         high = pltpu.roll(high, 16, 1)
         for bit in range(4):
             moved = lax.bitwise_and(shift, 1 << bit) != 0
@@ -350,16 +329,11 @@
             high = jnp.where(moved, pltpu.roll(high, 128 - (1 << bit), 1), high)
         window = jnp.where(in_group + shift < 16, low, high)
 
-        def body(i, tile):
-            for f in range(count):
-                for half in range(2):
-                    group = f * 2 + half
-                    ghosts[f, i, half * 8 : half * 8 + 8, :] = jnp.broadcast_to(
-                        tile[:, group * 16 : group * 16 + 1], (8, 128)
-                    )
-            return pltpu.roll(tile, 127, 1)
-
-        lax.fori_loop(0, cp, body, window)
+        for f in range(count):
+            for half in range(2):
+                for i in range(cp):
+                    spot = (f * 2 + half) * 16 + i
+                    ghosts[f, i, half * 8 : half * 8 + 8, :] = jnp.broadcast_to(window[:, spot : spot + 1], (8, 128))
 
     ghost(0, 4)
     lanes = iota((cr, ca), 1)
@@ -395,7 +369,7 @@
     no_inner = jnp.logical_and(hub, span_first)
     no_outer = jnp.logical_and(tip, span_last)
 
-    @pl.loop(0, cp)
+    @pl.loop(0, cp, unroll=UNROLL)
     def _(i):
         k = state[3, i + 1]
         k_out, k_in, k_right, k_left = around(
@@ -426,7 +400,7 @@
         coef[6, i] = jnp.where(no_west, 0.0, c_west)
 
     def advance(old, step, store):
-        @pl.loop(0, cp)
+        @pl.loop(0, cp, unroll=UNROLL)
         def _(i):
             c = [coef[n, i] for n in range(7)]
             for f in range(3):
@@ -448,8 +422,18 @@
     second = halo(state2, 1, 3)
     for copy in second:
         copy.start()
-    plane_send[1] = pack(lambda f, i, half: state2[min(f, 2), i + 1, pl.ds(half * 8, 8), pl.ds(offset, 128)])
-    spread_plane(1)
+    plane_send[1] = pack(3, lambda f, i, half: state2[f, i + 1, pl.ds(half * 8, 8), pl.ds(offset, 128)])
+    swap = swap_plane(1)
+    swap.start()
+
+    swap.wait()
+    spread_z(1)
+    drain(midway.at[0 : DEEP - 1], hand_sems, 0)
+    for step, peer in enumerate(x_peers):
+        far = wrap(x + step + 1, wide)
+        send(midway.at[:, far], landed.at[x], hand_sems, 2, (peer, s, q)).start()
+    landed[x] = midway[:, x]
+    spread_x(1)
     for copy in second:
         copy.wait()
     wait_plane(1)
@@ -460,12 +444,9 @@
 
     advance(state2, 1, store_second)
 
-    many = landed.at[0 : npitch - 1]
-    pltpu.make_async_copy(many, many, hand_sems.at[0]).wait()
-    pltpu.make_async_copy(many, many, hand_sems.at[1]).wait()
-
+    drain(landed.at[0 : wide - 1], hand_sems, 2)
     for d in range(npitch):
-        arrived_ref[:, d * 128 : (d + 1) * 128] = landed[d]
+        arrived_ref[:, d * 128 : (d + 1) * 128] = landed[d // DEEP, d % DEEP]
 
 
 def local(fields, diffusivity, mean_flow, radial_kernel, tracer_values, tracer_cells, tracer_dest, interface_map):
@@ -478,8 +459,8 @@
     return pl.pallas_call(
         functools.partial(kernel, npitch, nspan),
         out_shape=(
-            jax.ShapeDtypeStruct((3, 16, 16, 256), F32),
-            jax.ShapeDtypeStruct((10, npitch * 128), F32),
+            pltpu.VMEM((3, 16, 16, 256), F32),
+            pltpu.VMEM((10, npitch * 128), F32),
         ),
         in_specs=[anywhere] * 7 + [pl.BlockSpec(memory_space=pltpu.SMEM)],
         out_specs=(vmem, vmem),
@@ -496,17 +477,19 @@
             pltpu.VMEM((2, 2, 4, 16, 256), F32),
             pltpu.VMEM((2, 2, 4, 16, 256), F32),
             pltpu.VMEM((2, 8, 128), F32),
-            pltpu.VMEM((npitch, 8, 128), F32),
-            pltpu.VMEM((npitch, 8, 128), F32),
+            pltpu.VMEM((2, 8, 128), F32),
+            pltpu.VMEM((npitch // DEEP, DEEP, 8, 128), F32),
+            pltpu.VMEM((npitch // DEEP, DEEP, 8, 128), F32),
             pltpu.VMEM((16, 128), F32),
             pltpu.VMEM((16, 128), F32),
-            pltpu.VMEM((npitch, 10, 128), F32),
-            pltpu.VMEM((npitch, 10, 128), F32),
+            pltpu.VMEM((DEEP, npitch // DEEP, 10, 128), F32),
+            pltpu.VMEM((DEEP, npitch // DEEP, 10, 128), F32),
+            pltpu.VMEM((npitch // DEEP, DEEP, 10, 128), F32),
             pltpu.VMEM((2, 3, 256, 256), BF16),
             pltpu.VMEM((8, tracers), F32),
             pltpu.VMEM((8, tracers), F32),
             pltpu.VMEM((npitch, 1), F32),
-            pltpu.VMEM((npitch * 16, 128), F32),
+            pltpu.VMEM((npitch * 8, 256), F32),
             pltpu.VMEM((2, 16, 256), F32),
             pltpu.VMEM((7, 16, 16, 256), F32),
             pltpu.VMEM((4, 16, 16, 128), F32),
@@ -514,9 +497,9 @@
             dma((2,)),
             dma((2, 4)),
             dma((2, 4)),
-            dma((2, 2)),
+            dma((2, 6)),
             dma((2,)),
-            dma((2,)),
+            dma((4,)),
         ],
         compiler_params=pltpu.CompilerParams(
             collective_id=0, has_side_effects=True, vmem_limit_bytes=60 * 1024 * 1024

time: 49.9 us -> 40.4 us (0.81)
  Pallas kernels: 46.2 us -> 38 us
  local copies, waits for them, and re-layouts: 2.81 us -> 1.58 us
    pallas_call x1, Pallas kernels: 46.2 us -> 38 us  [local(): pl.pallas_call(functools.partial(kernel, npitch, nspan), out_shape=(pltpu...]
    unnamed x4 -> x2, local copies, waits for them, and re-layouts: 2.81 us -> 1.58 us
where the time goes in v2:
time: 40.4 us; the launch traced here: 40.2 us
  Pallas kernels  38 us (94%)
  local copies, waits for them, and re-layouts  1.58 us (4%)
  between operations  0.64 us (2%)
    pallas_call x1, Pallas kernels, local(): pl.pallas_call(functools.partial(kernel, npitch, nspan), out_shape=(pltpu...  38 us
    unnamed x2, local copies, waits for them, and re-layouts  1.58 us

profile of v2, /device:TPU:1, one launch (start us, length us, event | category | flops | bytes accessed | tf_op | source)
XLA Modules:
  0.0 40.2 jit_solution(16805604629908688233)
XLA Ops:
  0.6 38.0 %row_step.1 = (f32[3,16,16,256]{3,2,1,0:T(8,128)S(1)}, f32[10,4096]{1,0:T(8,128)S(1)}) custom-call(f32[3,16,16,256]{3,2,1,0:T(8,128)} %fields_hbm.1, f32[16,16,256]{2,1,0:T(8,128)} %kappa_hbm.1, bf16[16,2,256]{2,1,0:T(2,128)(2,1)} %flow_hbm.1, bf16[128,128]{1,0:T(8,128)(2,1)} %radial_hbm.1, f32[10,2048]{1,0:T(8,128)} %values_hbm.1, s32[1,2048]{1,0:T(1,128)} %bitcast.2, ...), custom_call_target="tpu_custom_call" | custom-call | tf_op jit(solution)/shard_map/row_step/pallas_call | solution.py:459
  38.7 0.9 %copy.12 = f32[3,16,16,256]{3,2,1,0:T(8,128)} copy(f32[3,16,16,256]{3,2,1,0:T(8,128)S(1)} %get-tuple-element.2) | data formatting | bytes 1572864
  39.5 0.7 %copy.13 = f32[10,4096]{1,0:T(8,128)} copy(f32[10,4096]{1,0:T(8,128)S(1)} %get-tuple-element.3) | data formatting | bytes 327680

commit v3 on v2

--- a/solution.py
+++ b/solution.py
@@ -60,7 +60,6 @@
     span_send,
     span_recv,
     plane_send,
-    plane_in,
     planes_first,
     planes_second,
     speed_send,
@@ -75,7 +74,6 @@
     hand,
     speeds,
     coef,
-    ghosts,
     load_sem,
     flow_sems,
     pitch_sems,
@@ -116,8 +114,9 @@
     span_peers = [wrap(s + step, nspan) for step in range(1, nspan)]
     up, down = wrap(p + 1, npitch), wrap(p + npitch - 1, npitch)
     outer, inner = wrap(s + 1, nspan), wrap(s + nspan - 1, nspan)
-    greeted = [(p, s, other), (up, s, q), (down, s, q)]
+    greeted = [(up, s, q), (down, s, q)]
     greeted += [(p, peer, q) for peer in span_peers]
+    greeted += [(peer, s, other) for peer in [p] + z_peers]
     greeted += [(peer, s, q) for peer in z_peers + x_peers]
     for device in greeted:
         pl.semaphore_signal(barrier, inc=1, device_id=device, device_id_type=MESH)
@@ -177,28 +176,23 @@
 
     planes = (planes_first, planes_second)
 
-    def swap_plane(step):
-        return send(plane_send.at[step], plane_in.at[step], plane_sems.at[step], 0, (p, s, other))
-
     def spread_z(step):
-        for peer in z_peers:
-            send(plane_in.at[step], planes[step].at[x, z], plane_sems.at[step], 2, (peer, s, q)).start()
-        planes[step][x, z] = plane_in[step]
+        for peer in [p] + z_peers:
+            send(plane_send.at[step], planes[step].at[x, z], plane_sems.at[step], 0, (peer, s, other)).start()
 
     def spread_x(step):
-        drain(planes[step].at[0, 0 : DEEP - 1], plane_sems.at[step], 2)
+        drain(planes[step].at[0], plane_sems.at[step], 0)
         for peer in x_peers:
-            send(planes[step].at[x], planes[step].at[x], plane_sems.at[step], 4, (peer, s, q)).start()
+            send(planes[step].at[x], planes[step].at[x], plane_sems.at[step], 2, (peer, s, q)).start()
 
     def wait_plane(step):
-        drain(planes[step].at[0 : wide - 1], plane_sems.at[step], 4)
+        drain(planes[step].at[0 : wide - 1], plane_sems.at[step], 2)
 
     loads[2].wait()
     loads[3].wait()
     plane_send[0] = pack(4, lambda f, i, half: state[f, i + 1, pl.ds(half * 8, 8), pl.ds(offset, 128)])
 
-    swap = swap_plane(0)
-    swap.start()
+    spread_z(0)
     first = halo(state, 0, 4)
     for copy in first[:2]:
         copy.start()
@@ -242,8 +236,6 @@
         counts[...] += jnp.sum(mine_f, axis=1, keepdims=True)
 
     sample(0)
-    swap.wait()
-    spread_z(0)
     sample(1)
     spread_x(0)
     sample(2)
@@ -308,10 +300,8 @@
         send(outgoing.at[far], midway.at[z], hand_sems, 0, (peer, s, q)).start()
     midway[z] = outgoing[z]
 
-    wait_plane(0)
     for copy in first:
         copy.wait()
-    speed_copy.wait()
 
     start_cell = map_ref[0, 0]
     facing = lax.shift_right_logical(start_cell, 4)
@@ -319,7 +309,7 @@
     facing_next = lax.bitwise_and(facing + 1, npitch - 1)
     in_group = lax.bitwise_and(lane, 15)
 
-    def ghost(step, count):
+    def facing_plane(step):
         low = planes[step][lax.shift_right_logical(facing, 3), lax.bitwise_and(facing, DEEP - 1)]
         high = planes[step][lax.shift_right_logical(facing_next, 3), lax.bitwise_and(facing_next, DEEP - 1)]
         high = pltpu.roll(high, 16, 1)
@@ -327,15 +317,17 @@
             moved = lax.bitwise_and(shift, 1 << bit) != 0
             low = jnp.where(moved, pltpu.roll(low, 128 - (1 << bit), 1), low)
             high = jnp.where(moved, pltpu.roll(high, 128 - (1 << bit), 1), high)
-        window = jnp.where(in_group + shift < 16, low, high)
-
-        for f in range(count):
+        return jnp.where(in_group + shift < 16, low, high)
+
+    def add_to_plane(ref, first_cell, delta):
+        for f in range(3):
             for half in range(2):
                 for i in range(cp):
                     spot = (f * 2 + half) * 16 + i
-                    ghosts[f, i, half * 8 : half * 8 + 8, :] = jnp.broadcast_to(window[:, spot : spot + 1], (8, 128))
-
-    ghost(0, 4)
+                    where = (f, i + first_cell, pl.ds(half * 8, 8), pl.ds(offset, 128))
+                    term = jnp.broadcast_to(delta[:, spot : spot + 1], (8, 128))
+                    ref[where] += jnp.where(near == 0, term, 0.0)
+
     lanes = iota((cr, ca), 1)
     radii = iota((cr, ca), 0)
     west, east = lanes == 0, lanes == ca - 1
@@ -344,25 +336,23 @@
     span_first = s == 0
     span_last = s == nspan - 1
 
-    def twice(x):
-        return jnp.concatenate([x, x], axis=1)
-
-    def around(x, inner_row, outer_row, ghost_tile):
+    def around(x, inner_row, outer_row):
         out = jnp.where(tip, outer_row, pltpu.roll(x, cr - 1, 0))
         inn = jnp.where(hub, inner_row, pltpu.roll(x, 1, 0))
-        right = jnp.where(east, ghost_tile, pltpu.roll(x, ca - 1, 1))
-        left = jnp.where(west, ghost_tile, pltpu.roll(x, 1, 1))
+        right = pltpu.roll(x, ca - 1, 1)
+        left = pltpu.roll(x, 1, 1)
         return out, inn, right, left
 
     sa = speeds[0]
     sp = speeds[1]
-    ghost_speed = twice(speed_recv[...])
     no_west = jnp.logical_and(west, stator)
     no_east = jnp.logical_and(east, jnp.logical_not(stator))
-    sa_right = jnp.where(no_east, sa, jnp.where(east, ghost_speed, pltpu.roll(sa, ca - 1, 1)))
-    sa_left = jnp.where(no_west, sa, jnp.where(west, ghost_speed, pltpu.roll(sa, 1, 1)))
-    w_east = 0.5 * (sa + sa_right)
-    w_west = 0.5 * (sa + sa_left)
+    east_open = jnp.where(jnp.logical_and(east, stator), 0.0, 1.0)
+    west_open = jnp.where(jnp.logical_and(west, jnp.logical_not(stator)), 0.0, 1.0)
+    sa_right = jnp.where(no_east, sa, pltpu.roll(sa, ca - 1, 1))
+    sa_left = jnp.where(no_west, sa, pltpu.roll(sa, 1, 1))
+    w_east = 0.5 * (sa + sa_right) * east_open
+    w_west = 0.5 * (sa + sa_left) * west_open
     ep, em = jnp.maximum(w_east, 0.0), jnp.minimum(w_east, 0.0)
     wp, wm = jnp.maximum(w_west, 0.0), jnp.minimum(w_west, 0.0)
     pp, pm = jnp.maximum(sp, 0.0), jnp.minimum(sp, 0.0)
@@ -373,7 +363,7 @@
     def _(i):
         k = state[3, i + 1]
         k_out, k_in, k_right, k_left = around(
-            k, span_recv[0, 0, 3, pl.ds(i, 1), :], span_recv[0, 1, 3, pl.ds(i, 1), :], twice(ghosts[3, i])
+            k, span_recv[0, 0, 3, pl.ds(i, 1), :], span_recv[0, 1, 3, pl.ds(i, 1), :]
         )
         k_right = jnp.where(no_east, k, k_right)
         k_left = jnp.where(no_west, k, k_left)
@@ -381,8 +371,8 @@
         d_down = 0.5 * (k + state[3, i])
         d_out = jnp.where(no_outer, 0.0, 0.5 * (k + k_out))
         d_in = jnp.where(no_inner, 0.0, 0.5 * (k + k_in))
-        d_east = 0.5 * (k + k_right)
-        d_west = 0.5 * (k + k_left)
+        d_east = 0.5 * (k + k_right) * east_open
+        d_west = 0.5 * (k + k_left) * west_open
         c_up = TIME_STEP * (d_up - pm)
         c_down = TIME_STEP * (d_down + pp)
         c_out = TIME_STEP * d_out
@@ -406,7 +396,7 @@
             for f in range(3):
                 v = old[f, i + 1]
                 out, inn, right, left = around(
-                    v, span_recv[step, 0, f, pl.ds(i, 1), :], span_recv[step, 1, f, pl.ds(i, 1), :], twice(ghosts[f, i])
+                    v, span_recv[step, 0, f, pl.ds(i, 1), :], span_recv[step, 1, f, pl.ds(i, 1), :]
                 )
                 new = c[0] * v + c[1] * old[f, i + 2] + c[2] * old[f, i]
                 new = new + c[3] * out + c[4] * inn + c[5] * right + c[6] * left
@@ -414,35 +404,60 @@
 
     def store_first(f, i, new):
         state2[f, i + 1] = new
-        span_send[1, 0, f, pl.ds(i, 1), :] = new[0:1, :]
-        span_send[1, 1, f, pl.ds(i, 1), :] = new[cr - 1 : cr, :]
 
     advance(state, 0, store_first)
+
+    base = pack(3, lambda f, i, half: state2[f, i + 1, pl.ds(half * 8, 8), pl.ds(offset, 128)])
+    plane_send[1] = base
+    spread_z(1)
+
+    wait_plane(0)
+    speed_copy.wait()
+    own = plane_send[0]
+    facing_own = facing_plane(0)
+    k_sum = 0.5 * (own + facing_own)
+    field = lax.shift_right_logical(lane, 5)
+    k_face = jnp.where(field == 0, pltpu.roll(k_sum, 32, 1), k_sum)
+    k_face = jnp.where(field == 1, pltpu.roll(k_sum, 64, 1), k_face)
+    k_face = jnp.where(field == 2, pltpu.roll(k_sum, 96, 1), k_face)
+    speed_sum = 0.5 * (speed_send[...] + speed_recv[...])
+    w_face = jnp.where(lax.bitwise_and(lane, 16) == 0, speed_sum[0:8], speed_sum[8:16])
+    w_plus, w_minus = jnp.maximum(w_face, 0.0), jnp.minimum(w_face, 0.0)
+    sign = jnp.where(q == 0, -TIME_STEP, TIME_STEP)
+
+    def change(mine, theirs):
+        lower = jnp.where(q == 0, mine, theirs)
+        upper = jnp.where(q == 0, theirs, mine)
+        return sign * (w_plus * lower + w_minus * upper - k_face * (upper - lower))
+
+    delta = change(own, facing_own)
+    add_to_plane(state2, 1, delta)
+
+    @pl.loop(0, cp)
+    def _(i):
+        for f in range(3):
+            span_send[1, 0, f, pl.ds(i, 1), :] = state2[f, i + 1, 0:1, :]
+            span_send[1, 1, f, pl.ds(i, 1), :] = state2[f, i + 1, cr - 1 : cr, :]
 
     second = halo(state2, 1, 3)
     for copy in second:
         copy.start()
-    plane_send[1] = pack(3, lambda f, i, half: state2[f, i + 1, pl.ds(half * 8, 8), pl.ds(offset, 128)])
-    swap = swap_plane(1)
-    swap.start()
-
-    swap.wait()
-    spread_z(1)
+
     drain(midway.at[0 : DEEP - 1], hand_sems, 0)
     for step, peer in enumerate(x_peers):
         far = wrap(x + step + 1, wide)
         send(midway.at[:, far], landed.at[x], hand_sems, 2, (peer, s, q)).start()
+    spread_x(1)
     landed[x] = midway[:, x]
-    spread_x(1)
     for copy in second:
         copy.wait()
-    wait_plane(1)
-    ghost(1, 3)
 
     def store_second(f, i, new):
         advected_ref[f, i] = new
 
     advance(state2, 1, store_second)
+    wait_plane(1)
+    add_to_plane(advected_ref, 0, change(base + delta, facing_plane(1) - delta))
 
     drain(landed.at[0 : wide - 1], hand_sems, 2)
     for d in range(npitch):
@@ -477,7 +492,6 @@
             pltpu.VMEM((2, 2, 4, 16, 256), F32),
             pltpu.VMEM((2, 2, 4, 16, 256), F32),
             pltpu.VMEM((2, 8, 128), F32),
-            pltpu.VMEM((2, 8, 128), F32),
             pltpu.VMEM((npitch // DEEP, DEEP, 8, 128), F32),
             pltpu.VMEM((npitch // DEEP, DEEP, 8, 128), F32),
             pltpu.VMEM((16, 128), F32),
@@ -492,12 +506,11 @@
             pltpu.VMEM((npitch * 8, 256), F32),
             pltpu.VMEM((2, 16, 256), F32),
             pltpu.VMEM((7, 16, 16, 256), F32),
-            pltpu.VMEM((4, 16, 16, 128), F32),
             dma((7,)),
             dma((2,)),
             dma((2, 4)),
             dma((2, 4)),
-            dma((2, 6)),
+            dma((2, 4)),
             dma((2,)),
             dma((4,)),
         ],

time: 40.4 us -> 39 us (0.965)
  Pallas kernels: 38 us -> 36.5 us
    pallas_call x1, Pallas kernels: 38 us -> 36.5 us  [local(): pl.pallas_call(functools.partial(kernel, npitch, nspan), out_shape=(pltpu...]
where the time goes in v3:
time: 39 us; the launch traced here: 38.8 us
  Pallas kernels  36.5 us (94%)
  local copies, waits for them, and re-layouts  1.58 us (4%)
  between operations  0.64 us (2%)
    pallas_call x1, Pallas kernels, local(): pl.pallas_call(functools.partial(kernel, npitch, nspan), out_shape=(pltpu...  36.5 us
    unnamed x2, local copies, waits for them, and re-layouts  1.58 us

profile of v3, /device:TPU:1, one launch (start us, length us, event | category | flops | bytes accessed | tf_op | source)
XLA Modules:
  0.0 38.8 jit_solution(15583517511484072810)
XLA Ops:
  0.6 36.5 %row_step.1 = (f32[3,16,16,256]{3,2,1,0:T(8,128)S(1)}, f32[10,4096]{1,0:T(8,128)S(1)}) custom-call(f32[3,16,16,256]{3,2,1,0:T(8,128)} %fields_hbm.1, f32[16,16,256]{2,1,0:T(8,128)} %kappa_hbm.1, bf16[16,2,256]{2,1,0:T(2,128)(2,1)} %flow_hbm.1, bf16[128,128]{1,0:T(8,128)(2,1)} %radial_hbm.1, f32[10,2048]{1,0:T(8,128)} %values_hbm.1, s32[1,2048]{1,0:T(1,128)} %bitcast.2, ...), custom_call_target="tpu_custom_call" | custom-call | tf_op jit(solution)/shard_map/row_step/pallas_call | solution.py:474
  37.2 0.9 %copy.12 = f32[3,16,16,256]{3,2,1,0:T(8,128)} copy(f32[3,16,16,256]{3,2,1,0:T(8,128)S(1)} %get-tuple-element.2) | data formatting | bytes 1572864
  38.1 0.7 %copy.13 = f32[10,4096]{1,0:T(8,128)} copy(f32[10,4096]{1,0:T(8,128)S(1)} %get-tuple-element.3) | data formatting | bytes 327680

commit v4 on v3

--- a/solution.py
+++ b/solution.py
@@ -65,7 +65,6 @@
     speed_send,
     speed_recv,
     outgoing,
-    midway,
     landed,
     fparts,
     sampled,
@@ -114,10 +113,9 @@
     span_peers = [wrap(s + step, nspan) for step in range(1, nspan)]
     up, down = wrap(p + 1, npitch), wrap(p + npitch - 1, npitch)
     outer, inner = wrap(s + 1, nspan), wrap(s + nspan - 1, nspan)
-    greeted = [(up, s, q), (down, s, q)]
-    greeted += [(p, peer, q) for peer in span_peers]
+    greeted = [(p, peer, q) for peer in span_peers]
     greeted += [(peer, s, other) for peer in [p] + z_peers]
-    greeted += [(peer, s, q) for peer in z_peers + x_peers]
+    greeted += [(wrap(p + far, npitch), s, q) for far in range(1, npitch)]
     for device in greeted:
         pl.semaphore_signal(barrier, inc=1, device_id=device, device_id_type=MESH)
 
@@ -294,11 +292,11 @@
         pass_on(chunk)
     for d in range(npitch):
         row, column = d // 2 * 16, d % 2 * 128
-        outgoing[d % DEEP, d // DEEP] = hand[row : row + 10, column : column + 128]
-    for step, peer in enumerate(z_peers):
-        far = wrap(z + step + 1, DEEP)
-        send(outgoing.at[far], midway.at[z], hand_sems, 0, (peer, s, q)).start()
-    midway[z] = outgoing[z]
+        outgoing[d] = hand[row : row + 10, column : column + 128]
+    for far in range(1, npitch):
+        to = wrap(p + far, npitch)
+        send(outgoing.at[to], landed.at[p], hand_sems, 0, (to, s, q)).start()
+    landed[p] = outgoing[p]
 
     for copy in first:
         copy.wait()
@@ -443,12 +441,7 @@
     for copy in second:
         copy.start()
 
-    drain(midway.at[0 : DEEP - 1], hand_sems, 0)
-    for step, peer in enumerate(x_peers):
-        far = wrap(x + step + 1, wide)
-        send(midway.at[:, far], landed.at[x], hand_sems, 2, (peer, s, q)).start()
     spread_x(1)
-    landed[x] = midway[:, x]
     for copy in second:
         copy.wait()
 
@@ -459,9 +452,9 @@
     wait_plane(1)
     add_to_plane(advected_ref, 0, change(base + delta, facing_plane(1) - delta))
 
-    drain(landed.at[0 : wide - 1], hand_sems, 2)
+    drain(landed.at[0 : npitch - 1], hand_sems, 0)
     for d in range(npitch):
-        arrived_ref[:, d * 128 : (d + 1) * 128] = landed[d // DEEP, d % DEEP]
+        arrived_ref[:, d * 128 : (d + 1) * 128] = landed[d]
 
 
 def local(fields, diffusivity, mean_flow, radial_kernel, tracer_values, tracer_cells, tracer_dest, interface_map):
@@ -496,9 +489,8 @@
             pltpu.VMEM((npitch // DEEP, DEEP, 8, 128), F32),
             pltpu.VMEM((16, 128), F32),
             pltpu.VMEM((16, 128), F32),
-            pltpu.VMEM((DEEP, npitch // DEEP, 10, 128), F32),
-            pltpu.VMEM((DEEP, npitch // DEEP, 10, 128), F32),
-            pltpu.VMEM((npitch // DEEP, DEEP, 10, 128), F32),
+            pltpu.VMEM((npitch, 10, 128), F32),
+            pltpu.VMEM((npitch, 10, 128), F32),
             pltpu.VMEM((2, 3, 256, 256), BF16),
             pltpu.VMEM((8, tracers), F32),
             pltpu.VMEM((8, tracers), F32),
@@ -512,7 +504,7 @@
             dma((2, 4)),
             dma((2, 4)),
             dma((2,)),
-            dma((4,)),
+            dma((2,)),
         ],
         compiler_params=pltpu.CompilerParams(
             collective_id=0, has_side_effects=True, vmem_limit_bytes=60 * 1024 * 1024

time: 39 us -> 39.3 us (level)
  no operation moved by 1% of the time
where the time goes in v4:
time: 39.3 us; the launch traced here: 39.1 us
  Pallas kernels  36.8 us (94%)
  local copies, waits for them, and re-layouts  1.58 us (4%)
  between operations  0.64 us (2%)
    pallas_call x1, Pallas kernels, local(): pl.pallas_call(functools.partial(kernel, npitch, nspan), out_shape=(pltpu...  36.8 us
    unnamed x2, local copies, waits for them, and re-layouts  1.58 us

profile of v4, /device:TPU:1, one launch (start us, length us, event | category | flops | bytes accessed | tf_op | source)
XLA Modules:
  0.0 39.1 jit_solution(12402290953853133486)
XLA Ops:
  0.6 36.8 %row_step.1 = (f32[3,16,16,256]{3,2,1,0:T(8,128)S(1)}, f32[10,4096]{1,0:T(8,128)S(1)}) custom-call(f32[3,16,16,256]{3,2,1,0:T(8,128)} %fields_hbm.1, f32[16,16,256]{2,1,0:T(8,128)} %kappa_hbm.1, bf16[16,2,256]{2,1,0:T(2,128)(2,1)} %flow_hbm.1, bf16[128,128]{1,0:T(8,128)(2,1)} %radial_hbm.1, f32[10,2048]{1,0:T(8,128)} %values_hbm.1, s32[1,2048]{1,0:T(1,128)} %bitcast.2, ...), custom_call_target="tpu_custom_call" | custom-call | tf_op jit(solution)/shard_map/row_step/pallas_call | solution.py:467
  37.5 0.9 %copy.12 = f32[3,16,16,256]{3,2,1,0:T(8,128)} copy(f32[3,16,16,256]{3,2,1,0:T(8,128)S(1)} %get-tuple-element.2) | data formatting | bytes 1572864
  38.4 0.7 %copy.13 = f32[10,4096]{1,0:T(8,128)} copy(f32[10,4096]{1,0:T(8,128)S(1)} %get-tuple-element.3) | data formatting | bytes 327680
